TPU v7x, 32 devices: a whole 2x2x4 slice. The times are simulated.
32 devices in a mesh: brick: 16 (over z, y, x), seed: 2 (over core).
Axes of the slice: x: 2, y: 2, z: 4, core: 2. Of those that a mesh axis runs over, the one named last changes fastest.
Arguments:
- seed_data: float32 [4, 65536], P(None, ('brick', 'seed')), as said below
- block_slot: int32 [512], replicated, may hold values from 0 to 511, as said below
- candidates: int32 [256, 8], P('brick', 'seed'), may hold values from 0 to 511, as said below
- cand_count: int32 [256], P('brick'), may hold values from 1 to 8
- pixel_mass: float32 [256, 512], P('brick'), may hold values from 0.1 to 1
Outputs:
- seed_stats: float32 [4, 65536], P(None, ('brick', 'seed'))
Inputs may be any that keep to these rules, and one draw needn't show every extreme that they name: A permutation of the storage positions. Block g is homed in brick g // 32 and stored on the device of brick index block_slot[g] // 32 and seed index (block_slot[g] // 16) % 2. For each brick and seed index, exactly 16 blocks homed in that brick are stored at that seed index; one device stores at most 1 block homed in any one brick, and some devices reach it. `candidates`: row t holds 8 distinct ids of blocks homed in tile t's brick, between (t // 16) * 32 and that plus 32 - 1. `seed_data`: the seeds of a block lie in the region of its home brick: second coordinate between h * 2 and (h + 1) * 2 for home brick h, first between 0 and 1, third between 0 and 8.
All inputs are finite; a program needn't handle non-finite values.
Results may differ from a plain program's by a relative error of at most 0.0003.
Values sent between devices are 32-bit elements; how exact they have to be, the bound alone decides.
No kernel may reach another device: no remote copies, remote signals or barrier semaphores. Data moves between devices by JAX's collectives and lax.ppermute only.
A program may use at most 64 MiB of HBM per device.

v0:
```python
import math

import jax
import jax.numpy as jnp
from jax import lax
from jax.sharding import PartitionSpec as P

TILES_Y = 2
TILES_Z = 8


blur_eps = 0.5
far_score = -1e30


def joined(value, axis, join):
    pieces = jax.tree.map(lambda part: lax.all_gather(part, axis), value)
    head = jax.tree.map(lambda part: part[0], pieces)
    tail = jax.tree.map(lambda part: part[1:], pieces)
    running, _ = lax.scan(lambda running, share: (join(running, share), None), head, tail)
    return running


def pixel_points(brick_ids, tile_ids):
    within = jnp.arange(512, dtype=jnp.int32)
    tile_x = tile_ids // (TILES_Y * TILES_Z)
    tile_y = tile_ids // TILES_Z % TILES_Y
    tile_z = tile_ids % TILES_Z
    offset_x = ((within // 64).astype(jnp.float32) + 0.5) / 8.0
    offset_y = ((within // 8 % 8).astype(jnp.float32) + 0.5) / 8.0
    offset_z = ((within % 8).astype(jnp.float32) + 0.5) / 8.0
    point_x = tile_x.astype(jnp.float32)[:, None] + offset_x[None, :]
    point_y = (brick_ids * TILES_Y + tile_y).astype(jnp.float32)[:, None] + offset_y[None, :]
    point_z = tile_z.astype(jnp.float32)[:, None] + offset_z[None, :]
    return jnp.stack([point_x, point_y, point_z])


def tile_scores(points, seed_cols, valid_cols):
    differ = points[0][:, :, None] - seed_cols[0][:, None, :]
    distance = differ * differ
    differ = points[1][:, :, None] - seed_cols[1][:, None, :]
    distance = distance + differ * differ
    differ = points[2][:, :, None] - seed_cols[2][:, None, :]
    distance = distance + differ * differ
    scores = (seed_cols[3][:, None, :] - distance) / blur_eps
    return jnp.where(valid_cols[:, None, :], scores, far_score)


def combine_stats(left_pair, right_pair):
    left_peak, left_total = left_pair
    right_peak, right_total = right_pair
    joint_peak = jnp.maximum(left_peak, right_peak)
    joint_total = left_total * jnp.exp(left_peak - joint_peak) + right_total * jnp.exp(
        right_peak - joint_peak
    )
    return (joint_peak, joint_total)


def body(seed_data, block_slot, candidates, cand_count, pixel_mass):
    brick_index = lax.axis_index("brick")
    shard_index = lax.axis_index("seed")
    brick_size = lax.axis_size("brick")
    seed_size = lax.axis_size("seed")
    lane_count = seed_data.shape[1] // 128
    home_blocks = lane_count * seed_size
    total_blocks = block_slot.shape[0]
    capacity = max(1, lane_count // brick_size)
    tile_count, slot_count = candidates.shape
    positions = jnp.arange(total_blocks, dtype=jnp.int32)
    inverse = jnp.zeros((total_blocks,), jnp.int32).at[block_slot].set(positions)
    home_of_pos = inverse // home_blocks
    grouped = home_of_pos.reshape(brick_size * seed_size, lane_count)
    lane_ids = jnp.arange(lane_count, dtype=jnp.int32)
    before = lane_ids[:, None] < lane_ids[None, :]
    same_home = grouped[:, :, None] == grouped[:, None, :]
    rank_of_pos = jnp.sum(same_home & before[None], axis=1).reshape(total_blocks)
    own_first = (brick_index * seed_size + shard_index) * lane_count
    own_home = lax.dynamic_slice_in_dim(home_of_pos, own_first, lane_count)
    own_rank = lax.dynamic_slice_in_dim(rank_of_pos, own_first, lane_count)
    own_seeds = seed_data.reshape(4, lane_count, 128)
    outgoing = jnp.zeros((4, brick_size * capacity, 128), jnp.float32)
    outgoing = outgoing.at[:, own_home * capacity + own_rank, :].set(own_seeds)
    incoming = lax.all_to_all(outgoing, "brick", split_axis=1, concat_axis=1, tiled=True)
    home_slots = lax.dynamic_slice_in_dim(block_slot, brick_index * home_blocks, home_blocks)
    home_shard = home_slots // lane_count % seed_size
    home_owner = home_slots // home_blocks
    home_rank = rank_of_pos[home_slots]
    home_flat = home_owner * capacity + home_rank
    members = jnp.arange(home_blocks, dtype=jnp.int32)
    earlier = members[:, None] < members[None, :]
    queue_pos = jnp.sum((home_shard[:, None] == home_shard[None, :]) & earlier, axis=0)
    panel_index = home_shard * lane_count + queue_pos
    is_mine = home_shard == shard_index
    target = jnp.where(is_mine, queue_pos, lane_count)
    compact = jnp.zeros((4, lane_count, 128), jnp.float32)
    compact = compact.at[:, target, :].set(incoming[:, home_flat, :], mode="drop")
    seed_panel = lax.all_gather(compact, "seed", axis=1, tiled=True)
    start_totals = jnp.zeros((4, home_blocks, 128), jnp.float32)
    group_size = math.gcd(tile_count, 8)
    step_count = tile_count // group_size
    slot_cols = slot_count * 128
    slot_ids = shard_index * slot_count + jnp.arange(slot_count, dtype=jnp.int32)
    cand_panel = panel_index[candidates - brick_index * home_blocks]
    valid_all = jnp.repeat(slot_ids[None, :] < cand_count[:, None], 128, axis=1)
    brick_ids = jnp.zeros((group_size,), jnp.int32) + brick_index

    def group_scores(step_index):
        first_tile = step_index * group_size
        tile_ids = first_tile + jnp.arange(group_size, dtype=jnp.int32)
        points = pixel_points(brick_ids, tile_ids)
        chosen = lax.dynamic_slice_in_dim(cand_panel, first_tile, group_size)
        seed_cols = seed_panel[:, chosen.reshape(-1), :].reshape(4, group_size, slot_cols)
        valid_cols = lax.dynamic_slice_in_dim(valid_all, first_tile, group_size)
        return (tile_scores(points, seed_cols, valid_cols), points, chosen, valid_cols)

    def local_both(step_index):
        scores, points, chosen, valid_cols = group_scores(step_index)
        pixel_peak = jnp.max(scores, axis=2)
        raw_share = jnp.where(valid_cols[:, None, :], jnp.exp(scores - pixel_peak[:, :, None]), 0.0)
        return (pixel_peak, jnp.sum(raw_share, axis=2))

    step_ids = jnp.arange(step_count, dtype=jnp.int32)
    peak_local, total_local = lax.map(local_both, step_ids)
    pixel_peak, pixel_total = joined((peak_local, total_local), "seed", combine_stats)

    def contribute(totals, step_bits):
        step_index, group_peak, group_total = step_bits
        scores, points, chosen, valid_cols = group_scores(step_index)
        raw_share = jnp.where(valid_cols[:, None, :], jnp.exp(scores - group_peak[:, :, None]), 0.0)
        shares = raw_share / group_total[:, :, None]
        pixel_weight = lax.dynamic_slice_in_dim(pixel_mass, step_index * group_size, group_size)
        features = jnp.stack(
            [
                pixel_weight,
                pixel_weight * points[0],
                pixel_weight * points[1],
                pixel_weight * points[2],
            ]
        )
        moments = jnp.einsum("fgi,gic->fgc", features, shares, precision=lax.Precision.HIGHEST)
        totals = totals.at[:, chosen.reshape(-1), :].add(
            moments.reshape(4, group_size * slot_count, 128)
        )
        return (totals, None)

    totals, unused = lax.scan(contribute, start_totals, (step_ids, pixel_peak, pixel_total))
    raw_target = home_owner * (seed_size * capacity) + home_shard * capacity + home_rank
    outgoing_raw = jnp.zeros((4, brick_size * seed_size * capacity, 128), jnp.float32)
    outgoing_raw = outgoing_raw.at[:, raw_target, :].set(totals[:, panel_index, :])
    arrived = lax.all_to_all(outgoing_raw, "brick", split_axis=1, concat_axis=1, tiled=True)
    arrived = arrived.reshape(4, brick_size, seed_size * capacity, 128)
    summed_raw = lax.psum_scatter(arrived, "seed", scatter_dimension=2, tiled=True)
    own_rows = summed_raw[:, own_home, own_rank, :]
    mass_row = own_rows[0]
    moment_rows = own_rows[1:4] - mass_row[None] * own_seeds[0:3]
    result = jnp.concatenate([mass_row[None], moment_rows], axis=0)
    return result.reshape(4, lane_count * 128)


def solution(mesh):
    placed = (P(None, ("brick", "seed")), P(), P("brick", "seed"), P("brick"), P("brick", None))
    return jax.shard_map(
        body, mesh=mesh, in_specs=placed, out_specs=P(None, ("brick", "seed")), check_vma=False
    )
```

profile of v0, /device:TPU:0, one launch (start us, length us, event | category | flops | bytes accessed | tf_op | source)
XLA Modules:
  0.0 127.0 jit_solution(10801698994256494854)
XLA Ops:
  6.5 0.7 compare_select_fusion.7
  7.2 2.4 %scatter_custom_fusion.1 = s32[512]{0:T(512)S(1)} fusion(s32[512]{0:T(512)S(1)} %compare_select_fusion.7, s32[512]{0:T(512)S(1)} %iota.132, s32[]{:T(128)} %constant.488.clone.1), kind=kCustom, calls=%fused_computation.207 | custom fusion | bytes 2052 | tf_op jit(solution)/shard_map/scatter | solution.py:70
  9.8 0.1 convert_reduce_fusion
  10.2 0.6 broadcast.1155.clone
  10.8 2.2 %scatter_fusion.1 = f32[4,16,128]{2,0,1:T(4,128)} fusion(f32[4,16,128]{2,0,1:T(4,128)} %broadcast.1155.clone, s32[16]{0:T(128)S(1)} %get-tuple-element.468, f32[16,4,128]{2,1,0:T(4,128)S(1)} %bitcast.70), kind=kCustom, calls=%fused_computation.9 | custom fusion | bytes 98368 | tf_op jit(solution)/shard_map/scatter | solution.py:82
  13.0 8.3 %all-to-all-start = ((f32[4,16,128]{2,0,1:T(4,128)}), f32[4,16,128]{2,0,1:T(4,128)S(1)}, u32[]{:S(2)}, u32[]{:S(2)}) async-start(f32[4,16,128]{2,0,1:T(4,128)} %scatter_fusion.1), calls=%async_computation | async-start | bytes 65536 | tf_op jit(solution)/shard_map/all_to_all | solution.py:83
  21.5 0.7 gather_fusion.2
  22.3 0.1 compare_select_fusion.14
  22.4 0.1 convert_reduce_fusion.1
  22.6 0.1 reshape.575
  22.7 0.8 gather_fusion.3
  23.8 4.9 %all-to-all-done = f32[4,16,128]{2,0,1:T(4,128)S(1)} async-done(((f32[4,16,128]{2,0,1:T(4,128)}), f32[4,16,128]{2,0,1:T(4,128)S(1)}, u32[]{:S(2)}, u32[]{:S(2)}) %all-to-all-start) | async-done | bytes 32800 | tf_op jit(solution)/shard_map/all_to_all | solution.py:83
  28.7 0.6 gather_fusion.4
  29.3 1.5 %scatter_fusion.2 = f32[4,16,128]{2,0,1:T(4,128)S(1)} fusion(f32[4,16,128]{2,0,1:T(4,128)S(1)} %broadcast.1155, s32[32]{0:T(128)S(1)} %get-tuple-element.469, f32[32,4,128]{2,1,0:T(4,128)S(1)} %gather_fusion.4), kind=kCustom, calls=%fused_computation.10 | custom fusion | bytes 196736 | tf_op jit(solution)/shard_map/scatter | solution.py:96
  30.9 1.9 %all_gather.15 = f32[4,32,128]{2,0,1:T(4,128)S(1)} all-gather(f32[4,16,128]{2,0,1:T(4,128)S(1)} %scatter_fusion.2), channel_id=1, replica_groups=mesh['brick'=16,'seed'=2] {'seed'}, dimensions={1}, use_global_device_ids=true | all-gather | bytes 98304 | tf_op jit(solution)/shard_map/all_gather | solution.py:97
  32.7 34.8 %while.35 = (s32[]{:T(128)}, f32[2,8,512]{2,1,0:T(8,128)S(1)}, f32[2,8,512]{2,1,0:T(8,128)S(1)}, s32[2]{0:T(128)S(1)}, pred[16,512]{1,0:T(8,128)(4,1)S(1)}, /*in...) while((s32[]{:T(128)}, f32[2,8,512]{2,1,0:T(8,128)S(1)}, ...), condition=%wide.region_8.9_spmd.clone, body=%wide.region_5.8_spmd.clone.sunk | while | flops 54553152 | bytes 820639 | solution.py:123
  32.7 0.6 dynamic_slice.117
  34.1 0.6 gather_fusion
  34.7 0.2 slice_reduce_fusion.10
  35.2 4.3 %fusion.113 = f32[8,512]{1,0:T(8,128)S(1)} fusion(f32[8,512]{1,0:T(8,128)S(1)} %sub.605, f32[8,512]{1,0:T(8,128)S(1)} %broadcast_add_fusion.9, f32[8,512]{1,0:T(8,128)S(1)} %sub.606, f32[8,512]{1,0:T(8,128)S(1)} %broadcast_add_fusion.10, f32[8,512]{1,0:T(8,128)S(1)} %sub.607, f32[8,512]{1,0:T(8,128)S(1)} %broadcast_add_fusion.11, ...), kind=kLoop, calls=%fused_computation.16.clone.1 | loop fusion | flops 25161728 | bytes 135168 | tf_op jit(solution)/shard_map/while/body/eval_jaxpr/reduce_max | solution.py:118
  39.6 10.5 %select_reduce_fusion.2 = f32[8,512]{1,0:T(8,128)S(1)} fusion(f32[8,512]{1,0:T(8,128)S(1)} %fusion.113, f32[8,512]{1,0:T(8,128)S(1)} %sub.605, f32[8,512]{1,0:T(8,128)S(1)} %broadcast_add_fusion.9, f32[8,512]{1,0:T(8,128)S(1)} %sub.606, f32[8,512]{1,0:T(8,128)S(1)} %broadcast_add_fusion.10, f32[8,512]{1,0:T(8,128)S(1)} %sub.607, ...), kind=kLoop, calls=%fused_computation.14.clone.1 | loop fusion | flops 29356032 | bytes 151552 | tf_op jit(solution)/shard_map/while/body/eval_jaxpr/reduce_sum | solution.py:120
  50.1 0.6 dynamic_slice.117
  51.5 0.6 gather_fusion
  52.1 0.2 slice_reduce_fusion.10
  52.6 4.3 %fusion.113 = f32[8,512]{1,0:T(8,128)S(1)} fusion(f32[8,512]{1,0:T(8,128)S(1)} %sub.605, f32[8,512]{1,0:T(8,128)S(1)} %broadcast_add_fusion.9, f32[8,512]{1,0:T(8,128)S(1)} %sub.606, f32[8,512]{1,0:T(8,128)S(1)} %broadcast_add_fusion.10, f32[8,512]{1,0:T(8,128)S(1)} %sub.607, f32[8,512]{1,0:T(8,128)S(1)} %broadcast_add_fusion.11, ...), kind=kLoop, calls=%fused_computation.16.clone.1 | loop fusion | flops 25161728 | bytes 135168 | tf_op jit(solution)/shard_map/while/body/eval_jaxpr/reduce_max | solution.py:118
  57.0 10.5 %select_reduce_fusion.2 = f32[8,512]{1,0:T(8,128)S(1)} fusion(f32[8,512]{1,0:T(8,128)S(1)} %fusion.113, f32[8,512]{1,0:T(8,128)S(1)} %sub.605, f32[8,512]{1,0:T(8,128)S(1)} %broadcast_add_fusion.9, f32[8,512]{1,0:T(8,128)S(1)} %sub.606, f32[8,512]{1,0:T(8,128)S(1)} %broadcast_add_fusion.10, f32[8,512]{1,0:T(8,128)S(1)} %sub.607, ...), kind=kLoop, calls=%fused_computation.14.clone.1 | loop fusion | flops 29356032 | bytes 151552 | tf_op jit(solution)/shard_map/while/body/eval_jaxpr/reduce_sum | solution.py:120
  67.5 1.9 %all-gather = f32[4,8,512]{2,1,0:T(8,128)S(1)} all-gather(f32[2,8,512]{2,1,0:T(8,128)S(1)} %get-tuple-element.337), channel_id=2, replica_groups=mesh['brick'=16,'seed'=2] {'seed'}, dimensions={0}, use_global_device_ids=true | all-gather | bytes 98304 | tf_op jit(solution)/shard_map/all_gather | solution.py:17
  69.3 1.8 %all-gather.1 = f32[4,8,512]{2,1,0:T(8,128)S(1)} all-gather(f32[2,8,512]{2,1,0:T(8,128)S(1)} %get-tuple-element.338), channel_id=3, replica_groups=mesh['brick'=16,'seed'=2] {'seed'}, dimensions={0}, use_global_device_ids=true | all-gather | bytes 98304 | tf_op jit(solution)/shard_map/all_gather | solution.py:17
  71.2 0.7 copy-done
  72.0 29.0 %while.36 = (s32[]{:T(128)}, f32[4,32,128]{2,0,1:T(4,128)S(1)}, s32[2]{0:T(128)S(1)}, s32[16,4]{1,0:T(8,128)S(1)}, pred[16,512]{1,0:T(8,128)(4,1)S(1)}, /*index=...) while((s32[]{:T(128)}, f32[4,32,128]{2,0,1:T(4,128)S(1)}, ...), condition=%wide.region_11.12_spmd.clone, body=%wide.region_9.11_spmd.clone.sunk | while | flops 130135552 | bytes 1242671 | solution.py:146
  72.0 0.6 dynamic_slice.121
  73.6 0.6 gather_fusion.1
  74.2 0.2 slice_reduce_fusion.11
  74.5 10.3 %fusion.120 = f32[8,512,4]{1,2,0:T(4,128)S(1)} fusion(f32[8,512]{1,0:T(8,128)S(1)} %get-tuple-element.609, f32[8,512]{1,0:T(8,128)S(1)} %get-tuple-element.610, f32[8,512]{1,0:T(8,128)S(1)} %sub.625, f32[8,512]{1,0:T(8,128)S(1)} %get-tuple-element.617, f32[8,512]{1,0:T(8,128)S(1)} %sub.626, f32[8,512]{1,0:T(8,128)S(1)} %get-tuple-element.619, ...), kind=kOutput, calls=%fused_computation.78.clone.1 | convolution fusion | flops 130072576 | bytes 282624 | tf_op jit(solution)/shard_map/while/body/eval_jaxpr/fgi,gic->fgc/dot_general | solution.py:140
  84.8 1.7 %scatter_fusion = f32[4,32,128]{2,0,1:T(4,128)S(1)} fusion(f32[4,32,128]{2,0,1:T(4,128)S(1)} %get-tuple-element.681, s32[32]{0:T(128)S(1)} %fusion.115, f32[32,4,128]{2,1,0:T(4,128)S(1)} %bitcast.65), kind=kCustom, calls=%fused_computation.7.clone.clone.1 | custom fusion | flops 16384 | bytes 196736 | tf_op jit(solution)/shard_map/while/body/eval_jaxpr/scatter-add | solution.py:141
  86.4 0.6 dynamic_slice.121
  88.1 0.6 gather_fusion.1
  88.7 0.2 slice_reduce_fusion.11
  89.0 10.3 %fusion.120 = f32[8,512,4]{1,2,0:T(4,128)S(1)} fusion(f32[8,512]{1,0:T(8,128)S(1)} %get-tuple-element.609, f32[8,512]{1,0:T(8,128)S(1)} %get-tuple-element.610, f32[8,512]{1,0:T(8,128)S(1)} %sub.625, f32[8,512]{1,0:T(8,128)S(1)} %get-tuple-element.617, f32[8,512]{1,0:T(8,128)S(1)} %sub.626, f32[8,512]{1,0:T(8,128)S(1)} %get-tuple-element.619, ...), kind=kOutput, calls=%fused_computation.78.clone.1 | convolution fusion | flops 130072576 | bytes 282624 | tf_op jit(solution)/shard_map/while/body/eval_jaxpr/fgi,gic->fgc/dot_general | solution.py:140
  99.3 1.6 %scatter_fusion = f32[4,32,128]{2,0,1:T(4,128)S(1)} fusion(f32[4,32,128]{2,0,1:T(4,128)S(1)} %get-tuple-element.681, s32[32]{0:T(128)S(1)} %fusion.115, f32[32,4,128]{2,1,0:T(4,128)S(1)} %bitcast.65), kind=kCustom, calls=%fused_computation.7.clone.clone.1 | custom fusion | flops 16384 | bytes 196736 | tf_op jit(solution)/shard_map/while/body/eval_jaxpr/scatter-add | solution.py:141
  100.9 0.6 gather_fusion.5
  101.6 1.5 %scatter_fusion.3 = f32[4,32,128]{2,0,1:T(4,128)S(1)} fusion(f32[4,32,128]{2,0,1:T(4,128)S(1)} %broadcast.1150, s32[32]{0:T(128)S(1)} %get-tuple-element.452, f32[32,4,128]{2,1,0:T(4,128)S(1)} %gather_fusion.5), kind=kCustom, calls=%fused_computation.11 | custom fusion | bytes 196736 | tf_op jit(solution)/shard_map/scatter | solution.py:149
  103.1 10.1 %all_to_all.10 = f32[4,32,128]{2,0,1:T(4,128)S(1)} all-to-all(f32[4,32,128]{2,0,1:T(4,128)S(1)} %scatter_fusion.3), channel_id=1, replica_groups=mesh['brick'=16,'seed'=2] {'brick'}, dimensions={1} | all-to-all | bytes 131072 | tf_op jit(solution)/shard_map/all_to_all | solution.py:150
  113.2 0.6 copy.38
  113.8 4.3 %reduce-scatter.2.cloned.1.call-done = f32[4,16,1,128]{3,1,0,2:T(8,128)} async-done(((f32[4,16,2,128]{3,1,0,2:T(8,128)}), f32[4,16,1,128]{3,1,0,2:T(8,128)}) %reduce-scatter.2.cloned.1.call-update) | async-done | bytes 32784 | tf_op jit(solution)/shard_map/reduce_scatter | solution.py:152
  118.1 0.8 copy.39
  118.9 0.6 gather_fusion.6
  119.5 0.6 maximum_bitcast_fusion
  (121 shorter events, 2.8 us)
Async XLA Ops:
  9.8 1.0 copy-start.1
  10.8 10.6 %copy-start.2 = (s32[512]{0:T(512)S(1)}, s32[512]{0:T(512)}, u32[]{:S(2)}) copy-start(s32[512]{0:T(512)} %param.10) | copy-start | bytes 6148
  13.0 15.7 %all-to-all-start = ((f32[4,16,128]{2,0,1:T(4,128)}), f32[4,16,128]{2,0,1:T(4,128)S(1)}, u32[]{:S(2)}, u32[]{:S(2)}) async-start(f32[4,16,128]{2,0,1:T(4,128)} %scatter_fusion.1), calls=%async_computation | async-start | bytes 65536 | tf_op jit(solution)/shard_map/all_to_all | solution.py:83
  21.3 96.8 %reduce-scatter.2.cloned.1.call-start = ((), (), s32[]{:S(2)}) async-start(), calls=%async_computation.3 | async-start | bytes 98304 | tf_op jit(solution)/shard_map/reduce_scatter | solution.py:152
  21.5 1.0 copy-start.3
  22.7 0.9 copy-start.4
  71.2 0.8 copy-start
Sparse Core Ops, SparseCore 0:
  113.9 4.1 reduce-scatter.1
where the time goes:
time: 127 us
  other arithmetic  36 us (28%)
  local copies, waits for them, and re-layouts  20.5 us (16%)
  matrix products  20.5 us (16%)
  blocking collectives  15.7 us (12%)
  between operations  13.6 us (11%)
  waiting for transfers between devices  9.24 us (7%)
  starting transfers between devices  8.35 us (7%)
  loops' own time  3.11 us (2%)
    reduce_sum x2, other arithmetic, local_both(): return (pixel_peak, jnp.sum(raw_share, axis=2))  21 us
    dot_general x2, matrix products, contribute(): jnp.einsum('fgi,gic->fgc', features, shares, precision=lax.Precision.HIGH...  20.5 us
    all_to_all x1, blocking collectives, body(): lax.all_to_all(outgoing_raw, 'brick', split_axis=1, concat_axis=1, tiled=...  10.1 us
    reduce_max x2, other arithmetic, local_both(): pixel_peak = jnp.max(scores, axis=2)  8.68 us
    all_to_all x1, starting transfers between devices, body(): lax.all_to_all(outgoing, 'brick', split_axis=1, concat_axis=1, tiled=True)  8.31 us
    all_to_all x1, waiting for transfers between devices, body(): lax.all_to_all(outgoing, 'brick', split_axis=1, concat_axis=1, tiled=True)  4.92 us
    reduce_scatter x1, waiting for transfers between devices, body(): lax.psum_scatter(arrived, 'seed', scatter_dimension=2, tiled=True)  4.3 us
    all_gather x2, blocking collectives, joined(): pieces = jax.tree.map(lambda part: lax.all_gather(part, axis), value)  3.69 us
  transfers between devices with their start and end apart: 2, of which 2 were waited for; matrix products, arithmetic and copies ran while one was open for 2% of the time, Pallas kernels for 0%

commit v1 on v0

v1 whole, which is shorter than its diff:
```python
import functools

import jax
import jax.numpy as jnp
from jax import lax
from jax.experimental import pallas as pl
from jax.experimental.pallas import tpu as pltpu
from jax.sharding import PartitionSpec as P

TILES_Y = 2
TILES_Z = 8

LOG2E = 1.4426950408889634
LIFT = 40.0
DEAD = -1e30
CHUNK = 4


def stored_lane(slots, home, lane_count, home_blocks, device_index):
    per_row = 128 // home_blocks
    row = slots[home // per_row : home // per_row + 1, :]
    lanes = lax.broadcasted_iota(jnp.int32, (1, 128), 1)
    shift = lane_count.bit_length() - 1
    first = (home % per_row) * home_blocks
    found = (row >> shift == device_index) & (lanes >= first) & (lanes < first + home_blocks)
    return jnp.max(jnp.where(found, row & (lane_count - 1), -1))


def pack_kernel(sizes, slots_ref, seeds_ref, out_ref):
    brick_size, seed_size, lane_count, home_blocks = sizes
    device_index = lax.axis_index("brick") * seed_size + lax.axis_index("seed")
    slots = slots_ref[...]
    for home in range(brick_size):
        lane = stored_lane(slots, home, lane_count, home_blocks, device_index)
        first = pl.multiple_of(jnp.maximum(lane, 0) * 128, 128)
        block = jnp.where(lane >= 0, seeds_ref[:, pl.ds(first, 128)], 0.0)
        for shard in range(seed_size):
            out_ref[home * seed_size + shard] = block


def place_kernel(sizes, slots_ref, partial_ref, out_ref):
    brick_size, seed_size, lane_count, home_blocks = sizes
    device_index = lax.axis_index("brick") * seed_size + lax.axis_index("seed")
    slots = slots_ref[...]
    for home in range(brick_size):
        lane = stored_lane(slots, home, lane_count, home_blocks, device_index)
        block = partial_ref[home * seed_size]
        for shard in range(1, seed_size):
            block = block + partial_ref[home * seed_size + shard]

        def store(lane=lane, block=block):
            first = pl.multiple_of(jnp.maximum(lane, 0) * 128, 128)
            out_ref[:, pl.ds(first, 128)] = block

        pl.when(lane >= 0)(store)


def split(value):
    high = value.astype(jnp.bfloat16)
    low = (value - high.astype(jnp.float32)).astype(jnp.bfloat16)
    return high, low


def main_kernel(tiles, source_ref, weight_ref, seeds_ref, out_ref, score_ref, za_ref, zs_ref, xy_ref):
    source_count = seeds_ref.shape[0]
    slot_count = source_ref.shape[1]
    chunk_count = source_count // CHUNK
    rows = tiles * 8
    first_tile = lax.axis_index("seed") * tiles
    tile_x = first_tile // (TILES_Y * TILES_Z)
    tile_y = lax.axis_index("brick") * TILES_Y + first_tile // TILES_Z % TILES_Y
    tile_z = first_tile % TILES_Z
    centre_x = tile_x.astype(jnp.float32) + 0.5
    centre_y = tile_y.astype(jnp.float32) + 0.5
    base_z = tile_z.astype(jnp.float32) + 0.5
    centre_z = base_z + lax.broadcasted_iota(jnp.int32, (tiles, 128), 0).astype(jnp.float32)
    step8 = (lax.broadcasted_iota(jnp.int32, (8, 128), 0).astype(jnp.float32) - 3.5) / 8.0

    sources = source_ref[...]
    slot_source = [jnp.broadcast_to(sources[:, k : k + 1], (tiles, 128)) for k in range(slot_count)]

    def near(block):
        off_x = jnp.clip(seeds_ref[block, 0:1, :] - centre_x, -8.0, 8.0)
        off_y = jnp.clip(seeds_ref[block, 1:2, :] - centre_y, -8.0, 8.0)
        return off_x, off_y

    def centre_scores(block, peak):
        off_x, off_y = near(block)
        off_z = seeds_ref[block, 2:3, :] - centre_z
        score = (seeds_ref[block, 3:4, :] - (off_x * off_x + off_y * off_y)) - off_z * off_z
        live = slot_source[0] == block
        for k in range(1, slot_count):
            live = live | (slot_source[k] == block)
        score = jnp.where(live, score, DEAD)
        score_ref[block] = score
        return jnp.maximum(peak, score)

    peak = lax.fori_loop(
        0, source_count, centre_scores, jnp.full((tiles, 128), DEAD, jnp.float32), unroll=8
    )
    peak = jnp.max(peak, axis=1, keepdims=True)

    def factors(chunk, totals):
        for i in range(CHUNK):
            block = chunk * CHUNK + i
            cols = slice(i * 128, (i + 1) * 128)
            off_x, off_y = near(block)
            base = (score_ref[block] - peak) * (2.0 * LOG2E) + LIFT * LOG2E
            slope_z = (seeds_ref[block, 2:3, :] - centre_z) * (4.0 * LOG2E)
            za = jnp.concatenate(
                [jnp.exp2(base[t : t + 1] + step8 * slope_z[t : t + 1]) for t in range(tiles)], axis=0
            )
            za_ref[block] = za
            high, low = split(za)
            zs_ref[chunk, 0:rows, cols] = high
            zs_ref[chunk, rows : 2 * rows, cols] = low
            slope_x = off_x * (4.0 * LOG2E)
            part_y = step8 * (off_y * (4.0 * LOG2E))
            xy = jnp.concatenate(
                [jnp.exp2(slope_x * ((ix - 3.5) / 8.0) + part_y) for ix in range(8)], axis=0
            )
            high, low = split(xy)
            xy_ref[chunk, 0:64, cols] = high
            xy_ref[chunk, 64:128, cols] = low
        return totals + lax.dot_general(
            zs_ref[chunk], xy_ref[chunk], (((1,), (1,)), ((), ())), preferred_element_type=jnp.float32
        )

    totals = lax.fori_loop(0, chunk_count, factors, jnp.zeros((2 * rows, 128), jnp.float32))
    totals = totals[0:rows] + totals[rows : 2 * rows]
    totals = totals + pltpu.roll(totals, 64, 1)
    ratio = weight_ref[...] / totals
    lanes = lax.broadcasted_iota(jnp.int32, (rows, 128), 1)
    step_x = (((lanes >> 3) & 7).astype(jnp.float32) - 3.5) / 8.0
    step_y = ((lanes & 7).astype(jnp.float32) - 3.5) / 8.0
    high, low = split(jnp.concatenate([ratio, ratio * step_x, ratio * step_y], axis=0))
    left = jnp.concatenate([high, low], axis=1)
    pixel_z = jnp.concatenate([step8 + (base_z + t) for t in range(tiles)], axis=0)

    def over_pixels(value):
        value = value.reshape(tiles, 8, 128)
        return jnp.sum(jnp.sum(value, axis=0), axis=0, keepdims=True)

    def moments(chunk, carry):
        right = xy_ref[chunk]
        pulled = jnp.dot(left, jnp.concatenate([right, right], axis=0), preferred_element_type=jnp.float32)
        for i in range(CHUNK):
            block = chunk * CHUNK + i
            cols = slice(i * 128, (i + 1) * 128)
            za = za_ref[block]
            share = za * pulled[0:rows, cols]
            mass = over_pixels(share)
            sum_z = over_pixels(share * pixel_z)
            sum_x = over_pixels(za * pulled[rows : 2 * rows, cols])
            sum_y = over_pixels(za * pulled[2 * rows : 3 * rows, cols])
            off_x, off_y = near(block)
            out_ref[block, 0:1, :] = mass
            out_ref[block, 1:2, :] = sum_x - off_x * mass
            out_ref[block, 2:3, :] = sum_y - off_y * mass
            out_ref[block, 3:4, :] = sum_z - seeds_ref[block, 2:3, :] * mass
        return carry

    lax.fori_loop(0, chunk_count, moments, 0)


def body(seed_data, block_slot, candidates, cand_count, pixel_mass):
    shard_index = lax.axis_index("seed")
    brick_size = lax.axis_size("brick")
    seed_size = lax.axis_size("seed")
    device_count = brick_size * seed_size
    lane_count = seed_data.shape[1] // 128
    home_blocks = lane_count * seed_size
    tile_count = candidates.shape[0]
    tiles = tile_count // seed_size
    assert tiles * seed_size == tile_count and TILES_Z % tiles == 0
    assert 128 % home_blocks == 0 and lane_count & (lane_count - 1) == 0
    assert device_count % CHUNK == 0
    sizes = (brick_size, seed_size, lane_count, home_blocks)
    vmem = pl.BlockSpec(memory_space=pltpu.VMEM)
    panel = jax.ShapeDtypeStruct((device_count, 4, 128), jnp.float32)
    params = pltpu.CompilerParams(vmem_limit_bytes=60 << 20)

    slots = block_slot.reshape(-1, 128)
    outgoing = pl.pallas_call(
        functools.partial(pack_kernel, sizes),
        out_shape=panel,
        in_specs=[vmem, vmem],
        out_specs=vmem,
        name="pack_seeds",
    )(slots, seed_data)
    incoming = lax.all_to_all(outgoing, ("brick", "seed"), split_axis=0, concat_axis=0, tiled=True)

    chosen = lax.all_gather(candidates, "seed", axis=1, tiled=True)
    first_tile = shard_index * tiles
    chosen = lax.dynamic_slice_in_dim(chosen, first_tile, tiles)
    counts = lax.dynamic_slice_in_dim(cand_count, first_tile, tiles)
    slot_ids = jnp.arange(chosen.shape[1], dtype=jnp.int32)
    source = jnp.where(slot_ids[None, :] < counts[:, None], block_slot[chosen] // lane_count, -1)
    weight = lax.dynamic_slice_in_dim(pixel_mass, first_tile, tiles)
    weight = weight.reshape(tiles, 64, 8).transpose(0, 2, 1).reshape(tiles * 8, 64)
    weight = jnp.concatenate([weight, weight], axis=1)

    partial = pl.pallas_call(
        functools.partial(main_kernel, tiles),
        out_shape=panel,
        in_specs=[vmem, vmem, vmem],
        out_specs=vmem,
        scratch_shapes=[
            pltpu.VMEM((device_count, tiles, 128), jnp.float32),
            pltpu.VMEM((device_count, tiles * 8, 128), jnp.float32),
            pltpu.VMEM((device_count // CHUNK, tiles * 16, CHUNK * 128), jnp.bfloat16),
            pltpu.VMEM((device_count // CHUNK, 128, CHUNK * 128), jnp.bfloat16),
        ],
        compiler_params=params,
        name="brick_moments",
    )(source, weight, incoming)
    returned = lax.all_to_all(partial, ("brick", "seed"), split_axis=0, concat_axis=0, tiled=True)
    return pl.pallas_call(
        functools.partial(place_kernel, sizes),
        out_shape=jax.ShapeDtypeStruct(seed_data.shape, jnp.float32),
        in_specs=[vmem, vmem],
        out_specs=vmem,
        name="place_stats",
    )(slots, returned)


def solution(mesh):
    placed = (P(None, ("brick", "seed")), P(), P("brick", "seed"), P("brick"), P("brick", None))
    return jax.shard_map(
        body, mesh=mesh, in_specs=placed, out_specs=P(None, ("brick", "seed")), check_vma=False
    )
```

time: 127 us -> 40.3 us (0.32)
  other arithmetic: 36 us -> 1.38 us
  matrix products: 20.5 us -> 0 us
  local copies, waits for them, and re-layouts: 20.5 us -> 4 us
  between operations: 13.6 us -> 0.04 us
  Pallas kernels: 0 us -> 12 us
  waiting for transfers between devices: 9.24 us -> 0.85 us
  loops' own time: 3.11 us -> 0 us
  blocking collectives: 15.7 us -> 14.3 us
    reduce_sum x4 -> x0, other arithmetic: 21.2 us -> none  [the longest x2 21 us: local_both(): return (pixel_peak, jnp.sum(raw_share, axis=2))]
    dot_general x2 -> x0, matrix products: 20.5 us -> none  [contribute(): jnp.einsum('fgi,gic->fgc', features, shares, precision=lax.Precision.HIGH...]
    pallas_call x0 -> x3, Pallas kernels: none -> 12 us  [the longest x1 5.63 us: body(): pl.pallas_call(functools.partial(main_kernel, tiles), out_shape=panel, in...]
    reduce_max x2 -> x0, other arithmetic: 8.68 us -> none  [local_both(): pixel_peak = jnp.max(scores, axis=2)]
    scatter x4 -> x0, local copies, waits for them, and re-layouts: 7.61 us -> none  [the longest x1 2.43 us: body(): jnp.zeros((total_blocks,), jnp.int32).at[block_slot].set(positions)]
    gather x10 -> x2, local copies, waits for them, and re-layouts: 5.81 us -> 0.87 us  [body(): block_slot[chosen] // lane_count]
    reduce_scatter x1 -> x0, waiting for transfers between devices: 4.3 us -> none  [body(): lax.psum_scatter(arrived, 'seed', scatter_dimension=2, tiled=True)]
    all_to_all x1, waiting for transfers between devices: 4.92 us -> 0.85 us  [body(): lax.all_to_all(outgoing, ('brick', 'seed'), split_axis=0, concat_axis=0,...]
  transfers between devices with their start and end apart: 2 -> 1, of which waited for: 2 -> 1; matrix products, arithmetic and copies ran while one was open for 2% -> 7% of each run, Pallas kernels for 0% -> 0%
where the time goes in v1:
time: 40.3 us; the launch traced here: 39.8 us
  blocking collectives  14.3 us (35%)
  Pallas kernels  12 us (30%)
  starting transfers between devices  7.3 us (18%)
  local copies, waits for them, and re-layouts  4 us (10%)
  other arithmetic  1.38 us (3%)
  waiting for transfers between devices  0.85 us (2%)
    all_to_all x1, blocking collectives, body(): lax.all_to_all(partial, ('brick', 'seed'), split_axis=0, concat_axis=0, t...  12.5 us
    all_to_all x1, starting transfers between devices, body(): lax.all_to_all(outgoing, ('brick', 'seed'), split_axis=0, concat_axis=0,...  7.3 us
    pallas_call x1, Pallas kernels, body(): pl.pallas_call(functools.partial(main_kernel, tiles), out_shape=panel, in...  5.63 us
    pallas_call x1, Pallas kernels, body(): pl.pallas_call(functools.partial(place_kernel, sizes), out_shape=jax.Shap...  4.69 us
    unnamed x12, local copies, waits for them, and re-layouts  2.71 us
    all_gather x1, blocking collectives, body(): chosen = lax.all_gather(candidates, 'seed', axis=1, tiled=True)  1.77 us
    pallas_call x1, Pallas kernels, body(): pl.pallas_call(functools.partial(pack_kernel, sizes), out_shape=panel, in...  1.66 us
    gather x2, local copies, waits for them, and re-layouts, body(): block_slot[chosen] // lane_count  0.87 us
  transfers between devices with their start and end apart: 1, of which 1 were waited for; matrix products, arithmetic and copies ran while one was open for 7% of the time, Pallas kernels for 0%

profile of v1, /device:TPU:0, one launch (start us, length us, event | category | flops | bytes accessed | tf_op | source)
XLA Modules:
  0.0 39.8 jit_solution(4776319088701596279)
XLA Ops:
  0.0 0.0 copy-start
  0.0 1.7 %pack_seeds.1 = f32[32,4,128]{2,1,0:T(4,128)} custom-call(s32[4,128]{1,0:T(4,128)} %bitcast.9, f32[4,2048]{1,0:T(4,128)} %seeds_ref.1), custom_call_target="tpu_custom_call" | custom-call | tf_op jit(solution)/shard_map/pack_seeds/pallas_call | solution.py:184
  1.7 7.3 %all-to-all-start = ((f32[32,4,128]{2,1,0:T(4,128)}), f32[32,4,128]{2,1,0:T(4,128)S(1)}, u32[]{:S(2)}, u32[]{:S(2)}) async-start(f32[32,4,128]{2,1,0:T(4,128)} %pack_seeds.1), calls=%async_computation | async-start | bytes 131072 | tf_op jit(solution)/shard_map/all_to_all | solution.py:191
  9.0 0.0 copy-start.3
  9.0 0.7 %copy-done.3 = s32[16,4]{0,1:T(4,128)S(1)} copy-done((s32[16,4]{0,1:T(4,128)S(1)}, s32[16,4]{0,1:T(4,128)}, u32[]{:S(2)}) %copy-start.3) | copy-done | bytes 280
  9.7 1.8 %all-gather = s32[2,4,16]{2,1,0:T(4,128)S(1)} all-gather(s32[1,4,16]{2,1,0:T(4,128)S(1)} %bitcast.14), channel_id=1, replica_groups=mesh['brick'=16,'seed'=2] {'seed'}, dimensions={0}, use_global_device_ids=true | all-gather | bytes 768 | tf_op jit(solution)/shard_map/all_gather | solution.py:193
  11.4 0.1 constant_dynamic-slice_fusion.1
  11.5 0.1 copy.11
  11.6 0.1 reshape.15
  11.7 0.0 copy-start.1
  11.7 0.7 %copy-done.1 = s32[512]{0:T(512)S(1)} copy-done((s32[512]{0:T(512)S(1)}, s32[512]{0:T(512)}, u32[]{:S(2)}) %copy-start.1) | copy-done | bytes 2072
  12.3 0.8 %gather_fusion = s32[64]{0:T(128)S(1)} fusion(s32[512]{0:T(512)S(1)} %copy-done.1, s32[1024]{0:T(1024)S(1)} %pad_clamp_fusion), kind=kCustom, calls=%fused_computation | custom fusion | bytes 768 | tf_op jit(solution)/shard_map/gather | solution.py:198
  13.1 0.0 copy-start.4
  13.1 0.1 reshape.14
  13.2 0.6 %copy-done.4 = s32[16]{0:T(128)S(1)} copy-done((s32[16]{0:T(128)S(1)}, s32[16]{0:T(128)}, u32[]{:S(2)}) %copy-start.4) | copy-done | bytes 88
  13.8 0.1 dynamic_slice.9
  13.9 0.7 %fusion.1.source_ref = s32[8,8]{1,0:T(8,128)} fusion(s32[8,8]{1,0:T(8,128)S(1)} %reshape.14, s32[8]{0:T(128)S(1)} %dynamic_slice.9), kind=kLoop, calls=%fused_computation.8 | loop fusion | flops 1088 | bytes 544 | tf_op jit(solution)/shard_map/jit(_where)/select_n | solution.py:198
  14.5 0.0 copy-done
  14.5 0.2 reshape.11
  14.7 0.1 copy.10
  14.8 0.7 %pad_maximum_fusion.weight_ref = f32[64,128]{1,0:T(8,128)} fusion(f32[64,64]{1,0:T(8,128)S(1)} %bitcast.12), kind=kLoop, calls=%fused_computation.1 | loop fusion | flops 8192 | bytes 49152 | tf_op jit(solution)/shard_map/concatenate | solution.py:201
  15.5 0.8 %all-to-all-done.seeds_ref = f32[32,4,128]{2,1,0:T(4,128)S(1)} async-done(((f32[32,4,128]{2,1,0:T(4,128)}), f32[32,4,128]{2,1,0:T(4,128)S(1)}, u32[]{:S(2)}, u32[]{:S(2)}) %all-to-all-start) | async-done | bytes 65568 | tf_op jit(solution)/shard_map/all_to_all | solution.py:191
  16.4 0.0 copy-start.2
  16.4 0.6 %copy-done.2 = f32[32,4,128]{2,1,0:T(4,128)} copy-done((f32[32,4,128]{2,1,0:T(4,128)}, f32[32,4,128]{2,1,0:T(4,128)S(1)}, u32[]{:S(2)}) %copy-start.2) | copy-done | bytes 65560
  17.0 5.6 %brick_moments.1 = f32[32,4,128]{2,1,0:T(4,128)} custom-call(s32[8,8]{1,0:T(8,128)} %fusion.1.source_ref, f32[64,128]{1,0:T(8,128)} %pad_maximum_fusion.weight_ref, f32[32,4,128]{2,1,0:T(4,128)} %copy-done.2), custom_call_target="tpu_custom_call" | custom-call | tf_op jit(solution)/shard_map/brick_moments/pallas_call | solution.py:203
  22.6 12.5 %all_to_all.10.partial_ref = f32[32,4,128]{2,1,0:T(4,128)} all-to-all(f32[32,4,128]{2,1,0:T(4,128)} %brick_moments.1), channel_id=1, replica_groups=mesh['brick'=16,'seed'=2] {'brick','seed'}, dimensions={0} | all-to-all | bytes 131072 | tf_op jit(solution)/shard_map/all_to_all | solution.py:217
  35.1 4.7 %place_stats.1 = f32[4,2048]{1,0:T(4,128)} custom-call(s32[4,128]{1,0:T(4,128)} %bitcast.10, f32[32,4,128]{2,1,0:T(4,128)} %all_to_all.10.partial_ref), custom_call_target="tpu_custom_call" | custom-call | tf_op jit(solution)/shard_map/place_stats/pallas_call | solution.py:218
  (3 shorter events, 0.0 us)
Async XLA Ops:
  0.0 14.5 %copy-start = (f32[16,512]{1,0:T(8,128)S(1)}, f32[16,512]{1,0:T(8,128)}, u32[]{:S(2)}) copy-start(f32[16,512]{1,0:T(8,128)} %param.9) | copy-start | bytes 98308
  1.7 14.7 %all-to-all-start = ((f32[32,4,128]{2,1,0:T(4,128)}), f32[32,4,128]{2,1,0:T(4,128)S(1)}, u32[]{:S(2)}, u32[]{:S(2)}) async-start(f32[32,4,128]{2,1,0:T(4,128)} %pack_seeds.1), calls=%async_computation | async-start | bytes 131072 | tf_op jit(solution)/shard_map/all_to_all | solution.py:191
  9.0 0.7 %copy-start.3 = (s32[16,4]{0,1:T(4,128)S(1)}, s32[16,4]{0,1:T(4,128)}, u32[]{:S(2)}) copy-start(s32[16,4]{0,1:T(4,128)} %param.7) | copy-start | bytes 772
  11.7 0.7 %copy-start.1 = (s32[512]{0:T(512)S(1)}, s32[512]{0:T(512)}, u32[]{:S(2)}) copy-start(s32[512]{0:T(512)} %param.6) | copy-start | bytes 6148
  13.1 0.7 %copy-start.4 = (s32[16]{0:T(128)S(1)}, s32[16]{0:T(128)}, u32[]{:S(2)}) copy-start(s32[16]{0:T(128)} %param.8) | copy-start | bytes 196
  16.4 0.6 %copy-start.2 = (f32[32,4,128]{2,1,0:T(4,128)}, f32[32,4,128]{2,1,0:T(4,128)S(1)}, u32[]{:S(2)}) copy-start(f32[32,4,128]{2,1,0:T(4,128)S(1)} %all-to-all-done.seeds_ref) | copy-start | bytes 196612

commit v2 on v1

--- a/solution.py
+++ b/solution.py
@@ -42,17 +42,17 @@
     brick_size, seed_size, lane_count, home_blocks = sizes
     device_index = lax.axis_index("brick") * seed_size + lax.axis_index("seed")
     slots = slots_ref[...]
-    for home in range(brick_size):
-        lane = stored_lane(slots, home, lane_count, home_blocks, device_index)
-        block = partial_ref[home * seed_size]
+    rows = lax.broadcasted_iota(jnp.int32, slots.shape, 0)
+    lanes = lax.broadcasted_iota(jnp.int32, slots.shape, 1)
+    home = (rows * 128 + lanes) >> (home_blocks.bit_length() - 1)
+    homes = [
+        jnp.max(jnp.where(slots == device_index * lane_count + lane, home, 0)) for lane in range(lane_count)
+    ]
+    for lane in range(lane_count):
+        block = partial_ref[homes[lane] * seed_size]
         for shard in range(1, seed_size):
-            block = block + partial_ref[home * seed_size + shard]
-
-        def store(lane=lane, block=block):
-            first = pl.multiple_of(jnp.maximum(lane, 0) * 128, 128)
-            out_ref[:, pl.ds(first, 128)] = block
-
-        pl.when(lane >= 0)(store)
+            block = block + partial_ref[homes[lane] * seed_size + shard]
+        out_ref[:, lane * 128 : (lane + 1) * 128] = block
 
 
 def split(value):
@@ -177,7 +177,8 @@
     assert device_count % CHUNK == 0
     sizes = (brick_size, seed_size, lane_count, home_blocks)
     vmem = pl.BlockSpec(memory_space=pltpu.VMEM)
-    panel = jax.ShapeDtypeStruct((device_count, 4, 128), jnp.float32)
+    panel = pltpu.VMEM((device_count, 4, 128), jnp.float32)
+    near = functools.partial(pltpu.with_memory_space_constraint, memory_space=pltpu.VMEM)
     params = pltpu.CompilerParams(vmem_limit_bytes=60 << 20)
 
     slots = block_slot.reshape(-1, 128)
@@ -213,7 +214,7 @@
         ],
         compiler_params=params,
         name="brick_moments",
-    )(source, weight, incoming)
+    )(near(source), near(weight), near(incoming))
     returned = lax.all_to_all(partial, ("brick", "seed"), split_axis=0, concat_axis=0, tiled=True)
     return pl.pallas_call(
         functools.partial(place_kernel, sizes),
@@ -221,7 +222,7 @@
         in_specs=[vmem, vmem],
         out_specs=vmem,
         name="place_stats",
-    )(slots, returned)
+    )(slots, near(returned))
 
 
 def solution(mesh):

time: 40.3 us -> 33.4 us (0.83)
  Pallas kernels: 12 us -> 7.32 us
  blocking collectives: 14.3 us -> 12.8 us
  other arithmetic: 1.38 us -> 0.17 us
  waiting for transfers between devices: 0.85 us -> 2.06 us
  local copies, waits for them, and re-layouts: 4 us -> 3.38 us
    pallas_call x1, Pallas kernels: 4.69 us -> 1.52 us  [body(): pl.pallas_call(functools.partial(place_kernel, sizes), out_shape=jax.Shap...]
    all_to_all x1, blocking collectives: 12.5 us -> 11 us  [body(): lax.all_to_all(partial, ('brick', 'seed'), split_axis=0, concat_axis=0, t...]
    pallas_call x1, Pallas kernels: 5.63 us -> 4.15 us  [body(): pl.pallas_call(functools.partial(main_kernel, tiles), out_shape=panel, in...]
    all_to_all x1, waiting for transfers between devices: 0.85 us -> 2.06 us  [body(): lax.all_to_all(outgoing, ('brick', 'seed'), split_axis=0, concat_axis=0,...]
    unnamed x12 -> x10, local copies, waits for them, and re-layouts: 2.71 us -> 2.08 us
    concatenate x1, other arithmetic: 0.71 us -> 0.08 us  [body(): weight = jnp.concatenate([weight, weight], axis=1)]
    select_n x1, other arithmetic: 0.66 us -> 0.07 us  [body(): jnp.where(slot_ids[None, :] < counts[:, None], block_slot[chosen] // lane...]
  transfers between devices with their start and end apart: 1 -> 1, of which waited for: 1 -> 1; matrix products, arithmetic and copies ran while one was open for 7% -> 5% of each run, Pallas kernels for 0% -> 0%
where the time goes in v2:
time: 33.4 us; the launch traced here: 33 us
  blocking collectives  12.8 us (38%)
  Pallas kernels  7.32 us (22%)
  starting transfers between devices  7.3 us (22%)
  local copies, waits for them, and re-layouts  3.38 us (10%)
  waiting for transfers between devices  2.06 us (6%)
    all_to_all x1, blocking collectives, body(): lax.all_to_all(partial, ('brick', 'seed'), split_axis=0, concat_axis=0, t...  11 us
    all_to_all x1, starting transfers between devices, body(): lax.all_to_all(outgoing, ('brick', 'seed'), split_axis=0, concat_axis=0,...  7.3 us
    pallas_call x1, Pallas kernels, body(): pl.pallas_call(functools.partial(main_kernel, tiles), out_shape=panel, in...  4.15 us
    unnamed x10, local copies, waits for them, and re-layouts  2.08 us
    all_to_all x1, waiting for transfers between devices, body(): lax.all_to_all(outgoing, ('brick', 'seed'), split_axis=0, concat_axis=0,...  2.06 us
    all_gather x1, blocking collectives, body(): chosen = lax.all_gather(candidates, 'seed', axis=1, tiled=True)  1.77 us
    pallas_call x1, Pallas kernels, body(): pl.pallas_call(functools.partial(pack_kernel, sizes), out_shape=panel, in...  1.65 us
    pallas_call x1, Pallas kernels, body(): pl.pallas_call(functools.partial(place_kernel, sizes), out_shape=jax.Shap...  1.52 us
  transfers between devices with their start and end apart: 1, of which 1 were waited for; matrix products, arithmetic and copies ran while one was open for 5% of the time, Pallas kernels for 0%

profile of v2, /device:TPU:0, one launch (start us, length us, event | category | flops | bytes accessed | tf_op | source)
XLA Modules:
  0.0 33.0 jit_solution(15825366632443421058)
XLA Ops:
  0.0 0.0 copy-start
  0.0 1.6 %pack_seeds.1 = f32[32,4,128]{2,1,0:T(4,128)} custom-call(s32[4,128]{1,0:T(4,128)} %bitcast.9, f32[4,2048]{1,0:T(4,128)} %seeds_ref.1), custom_call_target="tpu_custom_call" | custom-call | tf_op jit(solution)/shard_map/pack_seeds/pallas_call | solution.py:185
  1.7 7.3 %all-to-all-start = ((f32[32,4,128]{2,1,0:T(4,128)}), f32[32,4,128]{2,1,0:T(4,128)S(1)}, u32[]{:S(2)}, u32[]{:S(2)}) async-start(f32[32,4,128]{2,1,0:T(4,128)} %pack_seeds.1), calls=%async_computation | async-start | bytes 131072 | tf_op jit(solution)/shard_map/all_to_all | solution.py:192
  9.0 0.0 copy-start.2
  9.0 0.7 %copy-done.2 = s32[16,4]{0,1:T(4,128)S(1)} copy-done((s32[16,4]{0,1:T(4,128)S(1)}, s32[16,4]{0,1:T(4,128)}, u32[]{:S(2)}) %copy-start.2) | copy-done | bytes 280
  9.6 1.8 %all-gather = s32[2,4,16]{2,1,0:T(4,128)S(1)} all-gather(s32[1,4,16]{2,1,0:T(4,128)S(1)} %bitcast.14), channel_id=1, replica_groups=mesh['brick'=16,'seed'=2] {'seed'}, dimensions={0}, use_global_device_ids=true | all-gather | bytes 768 | tf_op jit(solution)/shard_map/all_gather | solution.py:194
  11.4 0.1 constant_dynamic-slice_fusion.1
  11.5 0.1 copy.11
  11.6 0.1 reshape.15
  11.6 0.0 copy-start.1
  11.7 0.7 %copy-done.1 = s32[512]{0:T(512)S(1)} copy-done((s32[512]{0:T(512)S(1)}, s32[512]{0:T(512)}, u32[]{:S(2)}) %copy-start.1) | copy-done | bytes 2072
  12.3 0.8 %gather_fusion = s32[64]{0:T(128)S(1)} fusion(s32[512]{0:T(512)S(1)} %copy-done.1, s32[1024]{0:T(1024)S(1)} %pad_clamp_fusion), kind=kCustom, calls=%fused_computation | custom fusion | bytes 768 | tf_op jit(solution)/shard_map/gather | solution.py:199
  13.1 0.0 copy-start.3
  13.1 0.1 reshape.14
  13.2 0.6 %copy-done.3 = s32[16]{0:T(128)S(1)} copy-done((s32[16]{0:T(128)S(1)}, s32[16]{0:T(128)}, u32[]{:S(2)}) %copy-start.3) | copy-done | bytes 88
  13.8 0.1 dynamic_slice.9
  13.9 0.1 fusion.1.source_ref
  13.9 0.0 copy-done
  13.9 0.2 reshape.11
  14.1 0.1 copy.10
  14.2 0.1 pad_maximum_fusion.weight_ref
  14.3 2.1 %all-to-all-done.seeds_ref = f32[32,4,128]{2,1,0:T(4,128)S(1)} async-done(((f32[32,4,128]{2,1,0:T(4,128)}), f32[32,4,128]{2,1,0:T(4,128)S(1)}, u32[]{:S(2)}, u32[]{:S(2)}) %all-to-all-start) | async-done | bytes 65568 | tf_op jit(solution)/shard_map/all_to_all | solution.py:192
  16.4 4.1 %brick_moments.1 = f32[32,4,128]{2,1,0:T(4,128)S(1)} custom-call(s32[8,8]{1,0:T(8,128)S(1)} %fusion.1.source_ref, f32[64,128]{1,0:T(8,128)S(1)} %pad_maximum_fusion.weight_ref, f32[32,4,128]{2,1,0:T(4,128)S(1)} %all-to-all-done.seeds_ref), custom_call_target="tpu_custom_call" | custom-call | tf_op jit(solution)/shard_map/brick_moments/pallas_call | solution.py:204
  20.5 11.0 %all_to_all.10.partial_ref = f32[32,4,128]{2,1,0:T(4,128)S(1)} all-to-all(f32[32,4,128]{2,1,0:T(4,128)S(1)} %brick_moments.1), channel_id=1, replica_groups=mesh['brick'=16,'seed'=2] {'brick','seed'}, dimensions={0} | all-to-all | bytes 131072 | tf_op jit(solution)/shard_map/all_to_all | solution.py:218
  31.5 1.5 %place_stats.1 = f32[4,2048]{1,0:T(4,128)} custom-call(s32[4,128]{1,0:T(4,128)} %bitcast.10, f32[32,4,128]{2,1,0:T(4,128)S(1)} %all_to_all.10.partial_ref), custom_call_target="tpu_custom_call" | custom-call | tf_op jit(solution)/shard_map/place_stats/pallas_call | solution.py:219
  (3 shorter events, 0.0 us)
Async XLA Ops:
  0.0 13.9 %copy-start = (f32[16,512]{1,0:T(8,128)S(1)}, f32[16,512]{1,0:T(8,128)}, u32[]{:S(2)}) copy-start(f32[16,512]{1,0:T(8,128)} %param.9) | copy-start | bytes 98308
  1.7 14.7 %all-to-all-start = ((f32[32,4,128]{2,1,0:T(4,128)}), f32[32,4,128]{2,1,0:T(4,128)S(1)}, u32[]{:S(2)}, u32[]{:S(2)}) async-start(f32[32,4,128]{2,1,0:T(4,128)} %pack_seeds.1), calls=%async_computation | async-start | bytes 131072 | tf_op jit(solution)/shard_map/all_to_all | solution.py:192
  9.0 0.7 %copy-start.2 = (s32[16,4]{0,1:T(4,128)S(1)}, s32[16,4]{0,1:T(4,128)}, u32[]{:S(2)}) copy-start(s32[16,4]{0,1:T(4,128)} %param.7) | copy-start | bytes 772
  11.6 0.7 %copy-start.1 = (s32[512]{0:T(512)S(1)}, s32[512]{0:T(512)}, u32[]{:S(2)}) copy-start(s32[512]{0:T(512)} %param.6) | copy-start | bytes 6148
  13.1 0.7 %copy-start.3 = (s32[16]{0:T(128)S(1)}, s32[16]{0:T(128)}, u32[]{:S(2)}) copy-start(s32[16]{0:T(128)} %param.8) | copy-start | bytes 196

commit v3 on v2

--- a/solution.py
+++ b/solution.py
@@ -38,20 +38,45 @@
             out_ref[home * seed_size + shard] = block
 
 
-def place_kernel(sizes, slots_ref, partial_ref, out_ref):
+def prepare_kernel(sizes, tiles, slots_ref, counts_ref, *refs):
     brick_size, seed_size, lane_count, home_blocks = sizes
-    device_index = lax.axis_index("brick") * seed_size + lax.axis_index("seed")
+    panels, (source_ref, homes_ref) = refs[:seed_size], refs[seed_size:]
+    brick_index = lax.axis_index("brick")
+    shard_index = lax.axis_index("seed")
+    shift = lane_count.bit_length() - 1
+    slot_count, tile_count = panels[0].shape
+
+    row = brick_index // (128 // home_blocks)
+    lanes = lax.broadcasted_iota(jnp.int32, (1, 128), 1)
+    ident = jnp.broadcast_to(row * 128 + lanes, (tiles, 128))
+    holder = jnp.broadcast_to(slots_ref[pl.ds(row, 1), :] >> shift, (tiles, 128))
+    mine = shard_index * tiles + lax.broadcasted_iota(jnp.int32, (tiles, tile_count), 0)
+    mine = mine == lax.broadcasted_iota(jnp.int32, (tiles, tile_count), 1)
+    counts = counts_ref[...]
+    for turn in range(seed_size):
+        shard = lax.rem(shard_index + turn, seed_size)
+        for k in range(slot_count):
+            chosen = jnp.where(shard * slot_count + k < counts, panels[turn][k : k + 1, :], -1)
+            chosen = jnp.where(mine, jnp.broadcast_to(chosen, (tiles, tile_count)), -1)
+            chosen = jnp.max(chosen, axis=1, keepdims=True)
+            source = jnp.max(jnp.where(ident == chosen, holder, -1), axis=1, keepdims=True)
+            source_ref[turn * slot_count + k] = jnp.broadcast_to(source, (tiles, 128))
+
     slots = slots_ref[...]
     rows = lax.broadcasted_iota(jnp.int32, slots.shape, 0)
     lanes = lax.broadcasted_iota(jnp.int32, slots.shape, 1)
     home = (rows * 128 + lanes) >> (home_blocks.bit_length() - 1)
-    homes = [
-        jnp.max(jnp.where(slots == device_index * lane_count + lane, home, 0)) for lane in range(lane_count)
-    ]
+    first = (brick_index * seed_size + shard_index) * lane_count
     for lane in range(lane_count):
-        block = partial_ref[homes[lane] * seed_size]
+        homes_ref[lane] = jnp.max(jnp.where(slots == first + lane, home, 0))
+
+
+def place_kernel(seed_size, homes_ref, partial_ref, out_ref):
+    for lane in range(out_ref.shape[1] // 128):
+        first = homes_ref[lane] * seed_size
+        block = partial_ref[first]
         for shard in range(1, seed_size):
-            block = block + partial_ref[homes[lane] * seed_size + shard]
+            block = block + partial_ref[first + shard]
         out_ref[:, lane * 128 : (lane + 1) * 128] = block
 
 
@@ -63,7 +88,7 @@
 
 def main_kernel(tiles, source_ref, weight_ref, seeds_ref, out_ref, score_ref, za_ref, zs_ref, xy_ref):
     source_count = seeds_ref.shape[0]
-    slot_count = source_ref.shape[1]
+    slot_count = source_ref.shape[0]
     chunk_count = source_count // CHUNK
     rows = tiles * 8
     first_tile = lax.axis_index("seed") * tiles
@@ -76,8 +101,7 @@
     centre_z = base_z + lax.broadcasted_iota(jnp.int32, (tiles, 128), 0).astype(jnp.float32)
     step8 = (lax.broadcasted_iota(jnp.int32, (8, 128), 0).astype(jnp.float32) - 3.5) / 8.0
 
-    sources = source_ref[...]
-    slot_source = [jnp.broadcast_to(sources[:, k : k + 1], (tiles, 128)) for k in range(slot_count)]
+    slot_source = [source_ref[k] for k in range(slot_count)]
 
     def near(block):
         off_x = jnp.clip(seeds_ref[block, 0:1, :] - centre_x, -8.0, 8.0)
@@ -129,7 +153,8 @@
     totals = lax.fori_loop(0, chunk_count, factors, jnp.zeros((2 * rows, 128), jnp.float32))
     totals = totals[0:rows] + totals[rows : 2 * rows]
     totals = totals + pltpu.roll(totals, 64, 1)
-    ratio = weight_ref[...] / totals
+    weight = weight_ref[...]
+    ratio = jnp.concatenate([weight, weight], axis=1) / totals
     lanes = lax.broadcasted_iota(jnp.int32, (rows, 128), 1)
     step_x = (((lanes >> 3) & 7).astype(jnp.float32) - 3.5) / 8.0
     step_y = ((lanes & 7).astype(jnp.float32) - 3.5) / 8.0
@@ -177,6 +202,7 @@
     assert device_count % CHUNK == 0
     sizes = (brick_size, seed_size, lane_count, home_blocks)
     vmem = pl.BlockSpec(memory_space=pltpu.VMEM)
+    smem = pl.BlockSpec(memory_space=pltpu.SMEM)
     panel = pltpu.VMEM((device_count, 4, 128), jnp.float32)
     near = functools.partial(pltpu.with_memory_space_constraint, memory_space=pltpu.VMEM)
     params = pltpu.CompilerParams(vmem_limit_bytes=60 << 20)
@@ -191,15 +217,21 @@
     )(slots, seed_data)
     incoming = lax.all_to_all(outgoing, ("brick", "seed"), split_axis=0, concat_axis=0, tiled=True)
 
-    chosen = lax.all_gather(candidates, "seed", axis=1, tiled=True)
-    first_tile = shard_index * tiles
-    chosen = lax.dynamic_slice_in_dim(chosen, first_tile, tiles)
-    counts = lax.dynamic_slice_in_dim(cand_count, first_tile, tiles)
-    slot_ids = jnp.arange(chosen.shape[1], dtype=jnp.int32)
-    source = jnp.where(slot_ids[None, :] < counts[:, None], block_slot[chosen] // lane_count, -1)
-    weight = lax.dynamic_slice_in_dim(pixel_mass, first_tile, tiles)
+    own = candidates.T
+    panels = [own]
+    for turn in range(1, seed_size):
+        pairs = [(shard, (shard - turn) % seed_size) for shard in range(seed_size)]
+        panels.append(lax.ppermute(own, "seed", pairs))
+    slot_total = own.shape[0] * seed_size
+    source, homes = pl.pallas_call(
+        functools.partial(prepare_kernel, sizes, tiles),
+        out_shape=(pltpu.VMEM((slot_total, tiles, 128), jnp.int32), pltpu.SMEM((lane_count,), jnp.int32)),
+        in_specs=[vmem] * (2 + seed_size),
+        out_specs=(vmem, smem),
+        name="prepare",
+    )(near(slots), near(cand_count.reshape(1, -1)), *[near(part) for part in panels])
+    weight = lax.dynamic_slice_in_dim(pixel_mass, shard_index * tiles, tiles)
     weight = weight.reshape(tiles, 64, 8).transpose(0, 2, 1).reshape(tiles * 8, 64)
-    weight = jnp.concatenate([weight, weight], axis=1)
 
     partial = pl.pallas_call(
         functools.partial(main_kernel, tiles),
@@ -217,12 +249,12 @@
     )(near(source), near(weight), near(incoming))
     returned = lax.all_to_all(partial, ("brick", "seed"), split_axis=0, concat_axis=0, tiled=True)
     return pl.pallas_call(
-        functools.partial(place_kernel, sizes),
+        functools.partial(place_kernel, seed_size),
         out_shape=jax.ShapeDtypeStruct(seed_data.shape, jnp.float32),
-        in_specs=[vmem, vmem],
+        in_specs=[smem, vmem],
         out_specs=vmem,
         name="place_stats",
-    )(slots, near(returned))
+    )(homes, near(returned))
 
 
 def solution(mesh):

time: 33.4 us -> 30.5 us (0.913)
  waiting for transfers between devices: 2.06 us -> 6.39 us
  blocking collectives: 12.8 us -> 9.1 us
  local copies, waits for them, and re-layouts: 3.38 us -> 0.34 us
  Pallas kernels: 7.32 us -> 6.69 us
    all_to_all x1, waiting for transfers between devices: 2.06 us -> 5.78 us  [body(): lax.all_to_all(outgoing, ('brick', 'seed'), split_axis=0, concat_axis=0,...]
    unnamed x10 -> x8, local copies, waits for them, and re-layouts: 2.08 us -> 0.07 us
    all_to_all x1, blocking collectives: 11 us -> 9.1 us  [body(): lax.all_to_all(partial, ('brick', 'seed'), split_axis=0, concat_axis=0, t...]
    all_gather x1 -> x0, blocking collectives: 1.77 us -> none  [body(): chosen = lax.all_gather(candidates, 'seed', axis=1, tiled=True)]
    gather x2 -> x0, local copies, waits for them, and re-layouts: 0.87 us -> none  [body(): block_slot[chosen] // lane_count]
    ppermute x0 -> x1, waiting for transfers between devices: none -> 0.61 us  [body(): panels.append(lax.ppermute(own, 'seed', pairs))]
    pallas_call x1 -> x2, Pallas kernels: 1.52 us -> 0.97 us  [the longest x1 0.63 us: body(): pl.pallas_call(functools.partial(place_kernel, seed_size), out_shape=jax....]
  transfers between devices with their start and end apart: 1 -> 2, of which waited for: 1 -> 2; matrix products, arithmetic and copies ran while one was open for 5% -> 1% of each run, Pallas kernels for 0% -> 1%
where the time goes in v3:
time: 30.5 us; the launch traced here: 30.2 us
  blocking collectives  9.1 us (30%)
  starting transfers between devices  7.61 us (25%)
  Pallas kernels  6.69 us (22%)
  waiting for transfers between devices  6.39 us (21%)
  local copies, waits for them, and re-layouts  0.34 us (1%)
    all_to_all x1, blocking collectives, body(): lax.all_to_all(partial, ('brick', 'seed'), split_axis=0, concat_axis=0, t...  9.1 us
    all_to_all x1, starting transfers between devices, body(): lax.all_to_all(outgoing, ('brick', 'seed'), split_axis=0, concat_axis=0,...  7.3 us
    all_to_all x1, waiting for transfers between devices, body(): lax.all_to_all(outgoing, ('brick', 'seed'), split_axis=0, concat_axis=0,...  5.78 us
    pallas_call x1, Pallas kernels, body(): pl.pallas_call(functools.partial(main_kernel, tiles), out_shape=panel, in...  4.07 us
    pallas_call x1, Pallas kernels, body(): pl.pallas_call(functools.partial(pack_kernel, sizes), out_shape=panel, in...  1.65 us
    pallas_call x1, Pallas kernels, body(): pl.pallas_call(functools.partial(place_kernel, seed_size), out_shape=jax....  0.63 us
    ppermute x1, waiting for transfers between devices, body(): panels.append(lax.ppermute(own, 'seed', pairs))  0.61 us
  transfers between devices with their start and end apart: 2, of which 2 were waited for; matrix products, arithmetic and copies ran while one was open for 1% of the time, Pallas kernels for 1%

profile of v3, /device:TPU:0, one launch (start us, length us, event | category | flops | bytes accessed | tf_op | source)
XLA Modules:
  0.0 30.2 jit_solution(4552008112295785372)
XLA Ops:
  0.0 0.0 copy-start
  0.0 1.7 %pack_seeds.1 = f32[32,4,128]{2,1,0:T(4,128)} custom-call(s32[4,128]{1,0:T(4,128)} %bitcast.6, f32[4,2048]{1,0:T(4,128)} %seeds_ref.1), custom_call_target="tpu_custom_call" | custom-call | tf_op jit(solution)/shard_map/pack_seeds/pallas_call | solution.py:211
  1.7 0.0 copy-start.2
  1.7 7.3 %all-to-all-start = ((f32[32,4,128]{2,1,0:T(4,128)}), f32[32,4,128]{2,1,0:T(4,128)S(1)}, u32[]{:S(2)}, u32[]{:S(2)}) async-start(f32[32,4,128]{2,1,0:T(4,128)} %pack_seeds.1), calls=%async_computation | async-start | bytes 131072 | tf_op jit(solution)/shard_map/all_to_all | solution.py:218
  9.0 0.0 copy-done.2
  9.0 0.3 %collective-permute-start = (s32[4,16]{1,0:T(4,128)S(1)}, s32[4,16]{1,0:T(4,128)S(1)}, u32[]{:S(2)}, u32[]{:S(2)}) collective-permute-start(s32[4,16]{1,0:T(4,128)S(1)} %bitcast.8), channel_id=1, source_target_pairs={{0,1},{1,0},{2,3},{3,2},{4,5},{5,4},{6,7},{7,6},{8,9},{9,8},{10,11... | collective-permute-start | bytes 776 | tf_op jit(solution)/shard_map/ppermute | solution.py:224
  9.3 0.0 copy-done
  9.3 0.2 reshape.14
  9.5 0.0 copy-start.1
  9.5 0.1 copy.6
  9.6 0.0 copy-start.3
  9.6 0.6 %collective-permute-done.refs_1_ = s32[4,16]{1,0:T(4,128)S(1)} collective-permute-done((s32[4,16]{1,0:T(4,128)S(1)}, s32[4,16]{1,0:T(4,128)S(1)}, u32[]{:S(2)}, u32[]{:S(2)}) %collective-permute-start) | collective-permute-done | bytes 288 | tf_op jit(solution)/shard_map/ppermute | solution.py:224
  10.2 0.0 copy-done.1
  10.2 0.1 copy-done.3
  10.2 0.3 %prepare.1 = (s32[8,8,128]{2,1,0:T(8,128)S(1)}, s32[16]{0:T(128)S(4)}) custom-call(s32[4,128]{1,0:T(4,128)S(1)} %bitcast.7, s32[1,16]{1,0:T(1,128)S(1)} %bitcast.10, s32[4,16]{1,0:T(4,128)S(1)} %bitcast.9, s32[4,16]{1,0:T(4,128)S(1)} %collective-permute-done.refs_1_), custom_call_target="tpu_custom_call" | custom-call | tf_op jit(solution)/shard_map/prepare/pallas_call | solution.py:226
  10.6 5.8 %all-to-all-done.seeds_ref = f32[32,4,128]{2,1,0:T(4,128)S(1)} async-done(((f32[32,4,128]{2,1,0:T(4,128)}), f32[32,4,128]{2,1,0:T(4,128)S(1)}, u32[]{:S(2)}, u32[]{:S(2)}) %all-to-all-start) | async-done | bytes 65568 | tf_op jit(solution)/shard_map/all_to_all | solution.py:218
  16.4 4.1 %brick_moments.1 = f32[32,4,128]{2,1,0:T(4,128)S(1)} custom-call(s32[8,8,128]{2,1,0:T(8,128)S(1)} %get-tuple-element.8.source_ref, f32[64,64]{1,0:T(8,128)S(1)} %bitcast.5, f32[32,4,128]{2,1,0:T(4,128)S(1)} %all-to-all-done.seeds_ref), custom_call_target="tpu_custom_call" | custom-call | tf_op jit(solution)/shard_map/brick_moments/pallas_call | solution.py:236
  20.5 9.1 %all_to_all.10.partial_ref = f32[32,4,128]{2,1,0:T(4,128)S(1)} all-to-all(f32[32,4,128]{2,1,0:T(4,128)S(1)} %brick_moments.1), channel_id=1, replica_groups=mesh['brick'=16,'seed'=2] {'brick','seed'}, dimensions={0} | all-to-all | bytes 131072 | tf_op jit(solution)/shard_map/all_to_all | solution.py:250
  29.6 0.6 %place_stats.1 = f32[4,2048]{1,0:T(4,128)} custom-call(s32[16]{0:T(128)S(4)} %get-tuple-element.7.homes_ref, f32[32,4,128]{2,1,0:T(4,128)S(1)} %all_to_all.10.partial_ref), custom_call_target="tpu_custom_call" | custom-call | tf_op jit(solution)/shard_map/place_stats/pallas_call | solution.py:251
  (1 shorter events, 0.0 us)
Async XLA Ops:
  0.0 9.3 %copy-start = (f32[16,512]{1,0:T(8,128)S(1)}, f32[16,512]{1,0:T(8,128)}, u32[]{:S(2)}) copy-start(f32[16,512]{1,0:T(8,128)} %param.9) | copy-start | bytes 98308
  1.7 7.3 %copy-start.2 = (s32[16,4]{0,1:T(4,128)S(1)}, s32[16,4]{0,1:T(4,128)}, u32[]{:S(2)}) copy-start(s32[16,4]{0,1:T(4,128)} %param.7) | copy-start | bytes 772
  1.7 14.7 %all-to-all-start = ((f32[32,4,128]{2,1,0:T(4,128)}), f32[32,4,128]{2,1,0:T(4,128)S(1)}, u32[]{:S(2)}, u32[]{:S(2)}) async-start(f32[32,4,128]{2,1,0:T(4,128)} %pack_seeds.1), calls=%async_computation | async-start | bytes 131072 | tf_op jit(solution)/shard_map/all_to_all | solution.py:218
  9.0 1.2 %collective-permute-start = (s32[4,16]{1,0:T(4,128)S(1)}, s32[4,16]{1,0:T(4,128)S(1)}, u32[]{:S(2)}, u32[]{:S(2)}) collective-permute-start(s32[4,16]{1,0:T(4,128)S(1)} %bitcast.8), channel_id=1, source_target_pairs={{0,1},{1,0},{2,3},{3,2},{4,5},{5,4},{6,7},{7,6},{8,9},{9,8},{10,11... | collective-permute-start | bytes 776 | tf_op jit(solution)/shard_map/ppermute | solution.py:224
  9.5 0.7 %copy-start.1 = (s32[512]{0:T(512)S(1)}, s32[512]{0:T(512)}, u32[]{:S(2)}) copy-start(s32[512]{0:T(512)} %param.6) | copy-start | bytes 6148
  9.6 0.7 %copy-start.3 = (s32[16]{0:T(128)S(1)}, s32[16]{0:T(128)}, u32[]{:S(2)}) copy-start(s32[16]{0:T(128)} %param.8) | copy-start | bytes 196

commit v4 on v3

--- a/solution.py
+++ b/solution.py
@@ -150,7 +150,7 @@
             zs_ref[chunk], xy_ref[chunk], (((1,), (1,)), ((), ())), preferred_element_type=jnp.float32
         )
 
-    totals = lax.fori_loop(0, chunk_count, factors, jnp.zeros((2 * rows, 128), jnp.float32))
+    totals = lax.fori_loop(0, chunk_count, factors, jnp.zeros((2 * rows, 128), jnp.float32), unroll=8)
     totals = totals[0:rows] + totals[rows : 2 * rows]
     totals = totals + pltpu.roll(totals, 64, 1)
     weight = weight_ref[...]
@@ -185,7 +185,7 @@
             out_ref[block, 3:4, :] = sum_z - seeds_ref[block, 2:3, :] * mass
         return carry
 
-    lax.fori_loop(0, chunk_count, moments, 0)
+    lax.fori_loop(0, chunk_count, moments, 0, unroll=8)
 
 
 def body(seed_data, block_slot, candidates, cand_count, pixel_mass):

time: 30.5 us -> 28.4 us (0.931)
  Pallas kernels: 6.69 us -> 4.65 us
    pallas_call x1, Pallas kernels: 4.07 us -> 2.03 us  [body(): pl.pallas_call(functools.partial(main_kernel, tiles), out_shape=panel, in...]
where the time goes in v4:
time: 28.4 us; the launch traced here: 28.1 us
  blocking collectives  9.1 us (32%)
  starting transfers between devices  7.61 us (27%)
  waiting for transfers between devices  6.39 us (22%)
  Pallas kernels  4.65 us (16%)
  local copies, waits for them, and re-layouts  0.34 us (1%)
    all_to_all x1, blocking collectives, body(): lax.all_to_all(partial, ('brick', 'seed'), split_axis=0, concat_axis=0, t...  9.1 us
    all_to_all x1, starting transfers between devices, body(): lax.all_to_all(outgoing, ('brick', 'seed'), split_axis=0, concat_axis=0,...  7.3 us
    all_to_all x1, waiting for transfers between devices, body(): lax.all_to_all(outgoing, ('brick', 'seed'), split_axis=0, concat_axis=0,...  5.78 us
    pallas_call x1, Pallas kernels, body(): pl.pallas_call(functools.partial(main_kernel, tiles), out_shape=panel, in...  2.03 us
    pallas_call x1, Pallas kernels, body(): pl.pallas_call(functools.partial(pack_kernel, sizes), out_shape=panel, in...  1.65 us
    pallas_call x1, Pallas kernels, body(): pl.pallas_call(functools.partial(place_kernel, seed_size), out_shape=jax....  0.63 us
    ppermute x1, waiting for transfers between devices, body(): panels.append(lax.ppermute(own, 'seed', pairs))  0.61 us
  transfers between devices with their start and end apart: 2, of which 2 were waited for; matrix products, arithmetic and copies ran while one was open for 1% of the time, Pallas kernels for 1%

profile of v4, /device:TPU:0, one launch (start us, length us, event | category | flops | bytes accessed | tf_op | source)
XLA Modules:
  0.0 28.1 jit_solution(10772461415953847581)
XLA Ops:
  0.0 0.0 copy-start
  0.0 1.7 %pack_seeds.1 = f32[32,4,128]{2,1,0:T(4,128)} custom-call(s32[4,128]{1,0:T(4,128)} %bitcast.6, f32[4,2048]{1,0:T(4,128)} %seeds_ref.1), custom_call_target="tpu_custom_call" | custom-call | tf_op jit(solution)/shard_map/pack_seeds/pallas_call | solution.py:211
  1.7 0.0 copy-start.2
  1.7 7.3 %all-to-all-start = ((f32[32,4,128]{2,1,0:T(4,128)}), f32[32,4,128]{2,1,0:T(4,128)S(1)}, u32[]{:S(2)}, u32[]{:S(2)}) async-start(f32[32,4,128]{2,1,0:T(4,128)} %pack_seeds.1), calls=%async_computation | async-start | bytes 131072 | tf_op jit(solution)/shard_map/all_to_all | solution.py:218
  9.0 0.0 copy-done.2
  9.0 0.3 %collective-permute-start = (s32[4,16]{1,0:T(4,128)S(1)}, s32[4,16]{1,0:T(4,128)S(1)}, u32[]{:S(2)}, u32[]{:S(2)}) collective-permute-start(s32[4,16]{1,0:T(4,128)S(1)} %bitcast.8), channel_id=1, source_target_pairs={{0,1},{1,0},{2,3},{3,2},{4,5},{5,4},{6,7},{7,6},{8,9},{9,8},{10,11... | collective-permute-start | bytes 776 | tf_op jit(solution)/shard_map/ppermute | solution.py:224
  9.3 0.0 copy-done
  9.3 0.2 reshape.14
  9.5 0.0 copy-start.1
  9.5 0.1 copy.6
  9.6 0.0 copy-start.3
  9.6 0.6 %collective-permute-done.refs_1_ = s32[4,16]{1,0:T(4,128)S(1)} collective-permute-done((s32[4,16]{1,0:T(4,128)S(1)}, s32[4,16]{1,0:T(4,128)S(1)}, u32[]{:S(2)}, u32[]{:S(2)}) %collective-permute-start) | collective-permute-done | bytes 288 | tf_op jit(solution)/shard_map/ppermute | solution.py:224
  10.2 0.0 copy-done.1
  10.2 0.1 copy-done.3
  10.2 0.3 %prepare.1 = (s32[8,8,128]{2,1,0:T(8,128)S(1)}, s32[16]{0:T(128)S(4)}) custom-call(s32[4,128]{1,0:T(4,128)S(1)} %bitcast.7, s32[1,16]{1,0:T(1,128)S(1)} %bitcast.10, s32[4,16]{1,0:T(4,128)S(1)} %bitcast.9, s32[4,16]{1,0:T(4,128)S(1)} %collective-permute-done.refs_1_), custom_call_target="tpu_custom_call" | custom-call | tf_op jit(solution)/shard_map/prepare/pallas_call | solution.py:226
  10.6 5.8 %all-to-all-done.seeds_ref = f32[32,4,128]{2,1,0:T(4,128)S(1)} async-done(((f32[32,4,128]{2,1,0:T(4,128)}), f32[32,4,128]{2,1,0:T(4,128)S(1)}, u32[]{:S(2)}, u32[]{:S(2)}) %all-to-all-start) | async-done | bytes 65568 | tf_op jit(solution)/shard_map/all_to_all | solution.py:218
  16.4 2.0 %brick_moments.1 = f32[32,4,128]{2,1,0:T(4,128)S(1)} custom-call(s32[8,8,128]{2,1,0:T(8,128)S(1)} %get-tuple-element.8.source_ref, f32[64,64]{1,0:T(8,128)S(1)} %bitcast.5, f32[32,4,128]{2,1,0:T(4,128)S(1)} %all-to-all-done.seeds_ref), custom_call_target="tpu_custom_call" | custom-call | tf_op jit(solution)/shard_map/brick_moments/pallas_call | solution.py:236
  18.4 9.1 %all_to_all.10.partial_ref = f32[32,4,128]{2,1,0:T(4,128)S(1)} all-to-all(f32[32,4,128]{2,1,0:T(4,128)S(1)} %brick_moments.1), channel_id=1, replica_groups=mesh['brick'=16,'seed'=2] {'brick','seed'}, dimensions={0} | all-to-all | bytes 131072 | tf_op jit(solution)/shard_map/all_to_all | solution.py:250
  27.5 0.6 %place_stats.1 = f32[4,2048]{1,0:T(4,128)} custom-call(s32[16]{0:T(128)S(4)} %get-tuple-element.7.homes_ref, f32[32,4,128]{2,1,0:T(4,128)S(1)} %all_to_all.10.partial_ref), custom_call_target="tpu_custom_call" | custom-call | tf_op jit(solution)/shard_map/place_stats/pallas_call | solution.py:251
  (1 shorter events, 0.0 us)
Async XLA Ops:
  0.0 9.3 %copy-start = (f32[16,512]{1,0:T(8,128)S(1)}, f32[16,512]{1,0:T(8,128)}, u32[]{:S(2)}) copy-start(f32[16,512]{1,0:T(8,128)} %param.9) | copy-start | bytes 98308
  1.7 7.3 %copy-start.2 = (s32[16,4]{0,1:T(4,128)S(1)}, s32[16,4]{0,1:T(4,128)}, u32[]{:S(2)}) copy-start(s32[16,4]{0,1:T(4,128)} %param.7) | copy-start | bytes 772
  1.7 14.7 %all-to-all-start = ((f32[32,4,128]{2,1,0:T(4,128)}), f32[32,4,128]{2,1,0:T(4,128)S(1)}, u32[]{:S(2)}, u32[]{:S(2)}) async-start(f32[32,4,128]{2,1,0:T(4,128)} %pack_seeds.1), calls=%async_computation | async-start | bytes 131072 | tf_op jit(solution)/shard_map/all_to_all | solution.py:218
  9.0 1.2 %collective-permute-start = (s32[4,16]{1,0:T(4,128)S(1)}, s32[4,16]{1,0:T(4,128)S(1)}, u32[]{:S(2)}, u32[]{:S(2)}) collective-permute-start(s32[4,16]{1,0:T(4,128)S(1)} %bitcast.8), channel_id=1, source_target_pairs={{0,1},{1,0},{2,3},{3,2},{4,5},{5,4},{6,7},{7,6},{8,9},{9,8},{10,11... | collective-permute-start | bytes 776 | tf_op jit(solution)/shard_map/ppermute | solution.py:224
  9.5 0.7 %copy-start.1 = (s32[512]{0:T(512)S(1)}, s32[512]{0:T(512)}, u32[]{:S(2)}) copy-start(s32[512]{0:T(512)} %param.6) | copy-start | bytes 6148
  9.6 0.7 %copy-start.3 = (s32[16]{0:T(128)S(1)}, s32[16]{0:T(128)}, u32[]{:S(2)}) copy-start(s32[16]{0:T(128)} %param.8) | copy-start | bytes 196

commit v5 on v4

--- a/solution.py
+++ b/solution.py
@@ -26,14 +26,20 @@
     return jnp.max(jnp.where(found, row & (lane_count - 1), -1))
 
 
-def pack_kernel(sizes, slots_ref, seeds_ref, out_ref):
+def pack_kernel(sizes, slots_hbm, seeds_hbm, out_ref, slots_ref, seeds_ref, sems):
     brick_size, seed_size, lane_count, home_blocks = sizes
     device_index = lax.axis_index("brick") * seed_size + lax.axis_index("seed")
+    fetch_slots = pltpu.make_async_copy(slots_hbm, slots_ref, sems.at[0])
+    fetch_seeds = pltpu.make_async_copy(seeds_hbm, seeds_ref, sems.at[1])
+    fetch_slots.start()
+    fetch_seeds.start()
+    fetch_slots.wait()
     slots = slots_ref[...]
+    lanes = [stored_lane(slots, home, lane_count, home_blocks, device_index) for home in range(brick_size)]
+    fetch_seeds.wait()
     for home in range(brick_size):
-        lane = stored_lane(slots, home, lane_count, home_blocks, device_index)
-        first = pl.multiple_of(jnp.maximum(lane, 0) * 128, 128)
-        block = jnp.where(lane >= 0, seeds_ref[:, pl.ds(first, 128)], 0.0)
+        first = pl.multiple_of(jnp.maximum(lanes[home], 0) * 128, 128)
+        block = jnp.where(lanes[home] >= 0, seeds_ref[:, pl.ds(first, 128)], 0.0)
         for shard in range(seed_size):
             out_ref[home * seed_size + shard] = block
 
@@ -86,7 +92,7 @@
     return high, low
 
 
-def main_kernel(tiles, source_ref, weight_ref, seeds_ref, out_ref, score_ref, za_ref, zs_ref, xy_ref):
+def main_kernel(tiles, source_ref, weight_ref, seeds_ref, out_ref, score_ref, za_ref, zs_ref, xy_ref, lift_ref):
     source_count = seeds_ref.shape[0]
     slot_count = source_ref.shape[0]
     chunk_count = source_count // CHUNK
@@ -101,6 +107,8 @@
     centre_z = base_z + lax.broadcasted_iota(jnp.int32, (tiles, 128), 0).astype(jnp.float32)
     step8 = (lax.broadcasted_iota(jnp.int32, (8, 128), 0).astype(jnp.float32) - 3.5) / 8.0
 
+    shift_z = [jnp.exp2(step8 * (-4.0 * LOG2E * t)) for t in range(tiles)]
+
     slot_source = [source_ref[k] for k in range(slot_count)]
 
     def near(block):
@@ -129,20 +137,22 @@
             block = chunk * CHUNK + i
             cols = slice(i * 128, (i + 1) * 128)
             off_x, off_y = near(block)
-            base = (score_ref[block] - peak) * (2.0 * LOG2E) + LIFT * LOG2E
-            slope_z = (seeds_ref[block, 2:3, :] - centre_z) * (4.0 * LOG2E)
+            lift = jnp.exp2((score_ref[block] - peak) * (2.0 * LOG2E) + LIFT * LOG2E)
+            pull_z = jnp.exp2(step8 * ((seeds_ref[block, 2:3, :] - base_z) * (4.0 * LOG2E)))
             za = jnp.concatenate(
-                [jnp.exp2(base[t : t + 1] + step8 * slope_z[t : t + 1]) for t in range(tiles)], axis=0
+                [(pull_z * shift_z[t]) * lift[t : t + 1] for t in range(tiles)], axis=0
             )
             za_ref[block] = za
             high, low = split(za)
             zs_ref[chunk, 0:rows, cols] = high
             zs_ref[chunk, rows : 2 * rows, cols] = low
-            slope_x = off_x * (4.0 * LOG2E)
+            slope_x = off_x * (0.5 * LOG2E)
             part_y = step8 * (off_y * (4.0 * LOG2E))
-            xy = jnp.concatenate(
-                [jnp.exp2(slope_x * ((ix - 3.5) / 8.0) + part_y) for ix in range(8)], axis=0
-            )
+            grow = jnp.broadcast_to(jnp.exp2(slope_x), (8, 128))
+            plane = [jnp.exp2(part_y - 3.5 * slope_x)]
+            for ix in range(1, 8):
+                plane.append(plane[-1] * grow)
+            xy = jnp.concatenate(plane, axis=0)
             high, low = split(xy)
             xy_ref[chunk, 0:64, cols] = high
             xy_ref[chunk, 64:128, cols] = low
@@ -203,6 +213,7 @@
     sizes = (brick_size, seed_size, lane_count, home_blocks)
     vmem = pl.BlockSpec(memory_space=pltpu.VMEM)
     smem = pl.BlockSpec(memory_space=pltpu.SMEM)
+    hbm = pl.BlockSpec(memory_space=pltpu.HBM)
     panel = pltpu.VMEM((device_count, 4, 128), jnp.float32)
     near = functools.partial(pltpu.with_memory_space_constraint, memory_space=pltpu.VMEM)
     params = pltpu.CompilerParams(vmem_limit_bytes=60 << 20)
@@ -211,8 +222,13 @@
     outgoing = pl.pallas_call(
         functools.partial(pack_kernel, sizes),
         out_shape=panel,
-        in_specs=[vmem, vmem],
+        in_specs=[hbm, hbm],
         out_specs=vmem,
+        scratch_shapes=[
+            pltpu.VMEM(slots.shape, slots.dtype),
+            pltpu.VMEM(seed_data.shape, seed_data.dtype),
+            pltpu.SemaphoreType.DMA((2,)),
+        ],
         name="pack_seeds",
     )(slots, seed_data)
     incoming = lax.all_to_all(outgoing, ("brick", "seed"), split_axis=0, concat_axis=0, tiled=True)
@@ -243,6 +259,7 @@
             pltpu.VMEM((device_count, tiles * 8, 128), jnp.float32),
             pltpu.VMEM((device_count // CHUNK, tiles * 16, CHUNK * 128), jnp.bfloat16),
             pltpu.VMEM((device_count // CHUNK, 128, CHUNK * 128), jnp.bfloat16),
+            pltpu.VMEM((CHUNK, tiles, 128), jnp.float32),
         ],
         compiler_params=params,
         name="brick_moments",

time: 28.4 us -> 28.2 us (level)
  no operation moved by 1% of the time
where the time goes in v5:
time: 28.2 us; the launch traced here: 27.9 us
  blocking collectives  9.1 us (32%)
  starting transfers between devices  7.62 us (27%)
  waiting for transfers between devices  6.39 us (23%)
  Pallas kernels  4.4 us (16%)
  local copies, waits for them, and re-layouts  0.34 us (1%)
    all_to_all x1, blocking collectives, body(): lax.all_to_all(partial, ('brick', 'seed'), split_axis=0, concat_axis=0, t...  9.1 us
    all_to_all x1, starting transfers between devices, body(): lax.all_to_all(outgoing, ('brick', 'seed'), split_axis=0, concat_axis=0,...  7.3 us
    all_to_all x1, waiting for transfers between devices, body(): lax.all_to_all(outgoing, ('brick', 'seed'), split_axis=0, concat_axis=0,...  5.78 us
    pallas_call x1, Pallas kernels, body(): pl.pallas_call(functools.partial(main_kernel, tiles), out_shape=panel, in...  1.84 us
    pallas_call x1, Pallas kernels, body(): pl.pallas_call(functools.partial(pack_kernel, sizes), out_shape=panel, in...  1.59 us
    pallas_call x1, Pallas kernels, body(): pl.pallas_call(functools.partial(place_kernel, seed_size), out_shape=jax....  0.63 us
    ppermute x1, waiting for transfers between devices, body(): panels.append(lax.ppermute(own, 'seed', pairs))  0.61 us
  transfers between devices with their start and end apart: 2, of which 2 were waited for; matrix products, arithmetic and copies ran while one was open for 1% of the time, Pallas kernels for 1%

profile of v5, /device:TPU:0, one launch (start us, length us, event | category | flops | bytes accessed | tf_op | source)
XLA Modules:
  0.0 27.9 jit_solution(17443204347779300256)
XLA Ops:
  0.0 0.0 copy-start
  0.0 1.6 %pack_seeds.1 = f32[32,4,128]{2,1,0:T(4,128)} custom-call(s32[4,128]{1,0:T(4,128)} %bitcast.6, f32[4,2048]{1,0:T(4,128)} %seeds_hbm.1), custom_call_target="tpu_custom_call" | custom-call | tf_op jit(solution)/shard_map/pack_seeds/pallas_call | solution.py:222
  1.6 0.0 copy-start.2
  1.6 7.3 %all-to-all-start = ((f32[32,4,128]{2,1,0:T(4,128)}), f32[32,4,128]{2,1,0:T(4,128)S(1)}, u32[]{:S(2)}, u32[]{:S(2)}) async-start(f32[32,4,128]{2,1,0:T(4,128)} %pack_seeds.1), calls=%async_computation | async-start | bytes 131072 | tf_op jit(solution)/shard_map/all_to_all | solution.py:234
  8.9 0.0 copy-done.2
  8.9 0.3 %collective-permute-start = (s32[4,16]{1,0:T(4,128)S(1)}, s32[4,16]{1,0:T(4,128)S(1)}, u32[]{:S(2)}, u32[]{:S(2)}) collective-permute-start(s32[4,16]{1,0:T(4,128)S(1)} %bitcast.8), channel_id=1, source_target_pairs={{0,1},{1,0},{2,3},{3,2},{4,5},{5,4},{6,7},{7,6},{8,9},{9,8},{10,11... | collective-permute-start | bytes 776 | tf_op jit(solution)/shard_map/ppermute | solution.py:240
  9.2 0.0 copy-done
  9.3 0.2 reshape.14
  9.4 0.0 copy-start.1
  9.4 0.1 copy.6
  9.5 0.0 copy-start.3
  9.5 0.6 %collective-permute-done.refs_1_ = s32[4,16]{1,0:T(4,128)S(1)} collective-permute-done((s32[4,16]{1,0:T(4,128)S(1)}, s32[4,16]{1,0:T(4,128)S(1)}, u32[]{:S(2)}, u32[]{:S(2)}) %collective-permute-start) | collective-permute-done | bytes 288 | tf_op jit(solution)/shard_map/ppermute | solution.py:240
  10.2 0.0 copy-done.1
  10.2 0.1 copy-done.3
  10.2 0.3 %prepare.1 = (s32[8,8,128]{2,1,0:T(8,128)S(1)}, s32[16]{0:T(128)S(4)}) custom-call(s32[4,128]{1,0:T(4,128)S(1)} %bitcast.7, s32[1,16]{1,0:T(1,128)S(1)} %bitcast.10, s32[4,16]{1,0:T(4,128)S(1)} %bitcast.9, s32[4,16]{1,0:T(4,128)S(1)} %collective-permute-done.refs_1_), custom_call_target="tpu_custom_call" | custom-call | tf_op jit(solution)/shard_map/prepare/pallas_call | solution.py:242
  10.5 5.8 %all-to-all-done.seeds_ref = f32[32,4,128]{2,1,0:T(4,128)S(1)} async-done(((f32[32,4,128]{2,1,0:T(4,128)}), f32[32,4,128]{2,1,0:T(4,128)S(1)}, u32[]{:S(2)}, u32[]{:S(2)}) %all-to-all-start) | async-done | bytes 65568 | tf_op jit(solution)/shard_map/all_to_all | solution.py:234
  16.3 1.8 %brick_moments.1 = f32[32,4,128]{2,1,0:T(4,128)S(1)} custom-call(s32[8,8,128]{2,1,0:T(8,128)S(1)} %get-tuple-element.8.source_ref, f32[64,64]{1,0:T(8,128)S(1)} %bitcast.5, f32[32,4,128]{2,1,0:T(4,128)S(1)} %all-to-all-done.seeds_ref), custom_call_target="tpu_custom_call" | custom-call | tf_op jit(solution)/shard_map/brick_moments/pallas_call | solution.py:252
  18.2 9.1 %all_to_all.10.partial_ref = f32[32,4,128]{2,1,0:T(4,128)S(1)} all-to-all(f32[32,4,128]{2,1,0:T(4,128)S(1)} %brick_moments.1), channel_id=1, replica_groups=mesh['brick'=16,'seed'=2] {'brick','seed'}, dimensions={0} | all-to-all | bytes 131072 | tf_op jit(solution)/shard_map/all_to_all | solution.py:267
  27.3 0.6 %place_stats.1 = f32[4,2048]{1,0:T(4,128)} custom-call(s32[16]{0:T(128)S(4)} %get-tuple-element.7.homes_ref, f32[32,4,128]{2,1,0:T(4,128)S(1)} %all_to_all.10.partial_ref), custom_call_target="tpu_custom_call" | custom-call | tf_op jit(solution)/shard_map/place_stats/pallas_call | solution.py:268
  (1 shorter events, 0.0 us)
Async XLA Ops:
  0.0 9.2 %copy-start = (f32[16,512]{1,0:T(8,128)S(1)}, f32[16,512]{1,0:T(8,128)}, u32[]{:S(2)}) copy-start(f32[16,512]{1,0:T(8,128)} %param.9) | copy-start | bytes 98308
  1.6 7.3 %copy-start.2 = (s32[16,4]{0,1:T(4,128)S(1)}, s32[16,4]{0,1:T(4,128)}, u32[]{:S(2)}) copy-start(s32[16,4]{0,1:T(4,128)} %param.7) | copy-start | bytes 772
  1.6 14.7 %all-to-all-start = ((f32[32,4,128]{2,1,0:T(4,128)}), f32[32,4,128]{2,1,0:T(4,128)S(1)}, u32[]{:S(2)}, u32[]{:S(2)}) async-start(f32[32,4,128]{2,1,0:T(4,128)} %pack_seeds.1), calls=%async_computation | async-start | bytes 131072 | tf_op jit(solution)/shard_map/all_to_all | solution.py:234
  8.9 1.2 %collective-permute-start = (s32[4,16]{1,0:T(4,128)S(1)}, s32[4,16]{1,0:T(4,128)S(1)}, u32[]{:S(2)}, u32[]{:S(2)}) collective-permute-start(s32[4,16]{1,0:T(4,128)S(1)} %bitcast.8), channel_id=1, source_target_pairs={{0,1},{1,0},{2,3},{3,2},{4,5},{5,4},{6,7},{7,6},{8,9},{9,8},{10,11... | collective-permute-start | bytes 776 | tf_op jit(solution)/shard_map/ppermute | solution.py:240
  9.4 0.7 %copy-start.1 = (s32[512]{0:T(512)S(1)}, s32[512]{0:T(512)}, u32[]{:S(2)}) copy-start(s32[512]{0:T(512)} %param.6) | copy-start | bytes 6148
  9.5 0.7 %copy-start.3 = (s32[16]{0:T(128)S(1)}, s32[16]{0:T(128)}, u32[]{:S(2)}) copy-start(s32[16]{0:T(128)} %param.8) | copy-start | bytes 196

commit v6 on v5

--- a/solution.py
+++ b/solution.py
@@ -59,6 +59,7 @@
     mine = shard_index * tiles + lax.broadcasted_iota(jnp.int32, (tiles, tile_count), 0)
     mine = mine == lax.broadcasted_iota(jnp.int32, (tiles, tile_count), 1)
     counts = counts_ref[...]
+    words = [jnp.zeros((tiles, 128), jnp.int32)] * source_ref.shape[0]
     for turn in range(seed_size):
         shard = lax.rem(shard_index + turn, seed_size)
         for k in range(slot_count):
@@ -66,7 +67,12 @@
             chosen = jnp.where(mine, jnp.broadcast_to(chosen, (tiles, tile_count)), -1)
             chosen = jnp.max(chosen, axis=1, keepdims=True)
             source = jnp.max(jnp.where(ident == chosen, holder, -1), axis=1, keepdims=True)
-            source_ref[turn * slot_count + k] = jnp.broadcast_to(source, (tiles, 128))
+            source = jnp.broadcast_to(source, (tiles, 128))
+            bit = jnp.where(source >= 0, jnp.left_shift(1, source & 31), 0)
+            for word in range(len(words)):
+                words[word] = words[word] | jnp.where(source >> 5 == word, bit, 0)
+    for word in range(len(words)):
+        source_ref[word] = words[word]
 
     slots = slots_ref[...]
     rows = lax.broadcasted_iota(jnp.int32, slots.shape, 0)
@@ -92,9 +98,8 @@
     return high, low
 
 
-def main_kernel(tiles, source_ref, weight_ref, seeds_ref, out_ref, score_ref, za_ref, zs_ref, xy_ref, lift_ref):
+def main_kernel(tiles, source_ref, weight_ref, seeds_ref, out_ref, score_ref, zs_ref, xy_ref):
     source_count = seeds_ref.shape[0]
-    slot_count = source_ref.shape[0]
     chunk_count = source_count // CHUNK
     rows = tiles * 8
     first_tile = lax.axis_index("seed") * tiles
@@ -109,43 +114,38 @@
 
     shift_z = [jnp.exp2(step8 * (-4.0 * LOG2E * t)) for t in range(tiles)]
 
-    slot_source = [source_ref[k] for k in range(slot_count)]
 
     def near(block):
         off_x = jnp.clip(seeds_ref[block, 0:1, :] - centre_x, -8.0, 8.0)
         off_y = jnp.clip(seeds_ref[block, 1:2, :] - centre_y, -8.0, 8.0)
         return off_x, off_y
 
-    def centre_scores(block, peak):
-        off_x, off_y = near(block)
-        off_z = seeds_ref[block, 2:3, :] - centre_z
-        score = (seeds_ref[block, 3:4, :] - (off_x * off_x + off_y * off_y)) - off_z * off_z
-        live = slot_source[0] == block
-        for k in range(1, slot_count):
-            live = live | (slot_source[k] == block)
-        score = jnp.where(live, score, DEAD)
-        score_ref[block] = score
-        return jnp.maximum(peak, score)
-
-    peak = lax.fori_loop(
-        0, source_count, centre_scores, jnp.full((tiles, 128), DEAD, jnp.float32), unroll=8
-    )
+    def centre_scores(word, peak):
+        bits = source_ref[word]
+        for i in range(32):
+            block = word * 32 + i
+            off_x, off_y = near(block)
+            off_z = seeds_ref[block, 2:3, :] - centre_z
+            score = (seeds_ref[block, 3:4, :] - (off_x * off_x + off_y * off_y)) - off_z * off_z
+            score = jnp.where((bits >> i) & 1 == 1, score, DEAD)
+            score_ref[block] = score
+            peak = jnp.maximum(peak, score)
+        return peak
+
+    peak = lax.fori_loop(0, source_count // 32, centre_scores, jnp.full((tiles, 128), DEAD, jnp.float32))
     peak = jnp.max(peak, axis=1, keepdims=True)
 
     def factors(chunk, totals):
+        planes, columns = [], []
         for i in range(CHUNK):
             block = chunk * CHUNK + i
-            cols = slice(i * 128, (i + 1) * 128)
             off_x, off_y = near(block)
             lift = jnp.exp2((score_ref[block] - peak) * (2.0 * LOG2E) + LIFT * LOG2E)
             pull_z = jnp.exp2(step8 * ((seeds_ref[block, 2:3, :] - base_z) * (4.0 * LOG2E)))
-            za = jnp.concatenate(
-                [(pull_z * shift_z[t]) * lift[t : t + 1] for t in range(tiles)], axis=0
-            )
-            za_ref[block] = za
-            high, low = split(za)
-            zs_ref[chunk, 0:rows, cols] = high
-            zs_ref[chunk, rows : 2 * rows, cols] = low
+            za = jnp.concatenate([(pull_z * shift_z[t]) * lift[t : t + 1] for t in range(tiles)], axis=0)
+            both = jnp.concatenate(split(za), axis=0)
+            zs_ref[chunk, :, i * 128 : (i + 1) * 128] = both
+            columns.append(both)
             slope_x = off_x * (0.5 * LOG2E)
             part_y = step8 * (off_y * (4.0 * LOG2E))
             grow = jnp.broadcast_to(jnp.exp2(slope_x), (8, 128))
@@ -153,41 +153,47 @@
             for ix in range(1, 8):
                 plane.append(plane[-1] * grow)
             xy = jnp.concatenate(plane, axis=0)
-            high, low = split(xy)
-            xy_ref[chunk, 0:64, cols] = high
-            xy_ref[chunk, 64:128, cols] = low
-        return totals + lax.dot_general(
-            zs_ref[chunk], xy_ref[chunk], (((1,), (1,)), ((), ())), preferred_element_type=jnp.float32
+            xy_ref[block] = xy
+            planes.append(jnp.concatenate(split(xy), axis=0))
+        dot = functools.partial(
+            lax.dot_general, dimension_numbers=(((1,), (1,)), ((), ())), preferred_element_type=jnp.float32
         )
-
-    totals = lax.fori_loop(0, chunk_count, factors, jnp.zeros((2 * rows, 128), jnp.float32), unroll=8)
-    totals = totals[0:rows] + totals[rows : 2 * rows]
-    totals = totals + pltpu.roll(totals, 64, 1)
-    weight = weight_ref[...]
-    ratio = jnp.concatenate([weight, weight], axis=1) / totals
-    lanes = lax.broadcasted_iota(jnp.int32, (rows, 128), 1)
-    step_x = (((lanes >> 3) & 7).astype(jnp.float32) - 3.5) / 8.0
-    step_y = ((lanes & 7).astype(jnp.float32) - 3.5) / 8.0
-    high, low = split(jnp.concatenate([ratio, ratio * step_x, ratio * step_y], axis=0))
-    left = jnp.concatenate([high, low], axis=1)
-    pixel_z = jnp.concatenate([step8 + (base_z + t) for t in range(tiles)], axis=0)
-
-    def over_pixels(value):
-        value = value.reshape(tiles, 8, 128)
-        return jnp.sum(jnp.sum(value, axis=0), axis=0, keepdims=True)
+        half = CHUNK // 2
+        first = dot(jnp.concatenate(planes[:half], axis=1), jnp.concatenate(columns[:half], axis=1))
+        second = dot(jnp.concatenate(planes[half:], axis=1), jnp.concatenate(columns[half:], axis=1))
+        return totals[0] + first, totals[1] + second
+
+    totals = lax.fori_loop(0, chunk_count, factors, (jnp.zeros((128, 2 * rows), jnp.float32),) * 2, unroll=8)
+    totals = totals[0] + totals[1]
+    totals = totals[0:64] + totals[64:128]
+    totals = totals[:, 0:rows] + totals[:, rows : 2 * rows]
+    ratio = weight_ref[...] / totals
+    ratio = jnp.concatenate([ratio, ratio], axis=1)
+    lanes = lax.broadcasted_iota(jnp.int32, (64, 2 * rows), 1) & (rows - 1)
+    pixel_z = base_z + (lanes >> 3).astype(jnp.float32) + ((lanes & 7).astype(jnp.float32) - 3.5) / 8.0
+    left = jnp.concatenate(split(jnp.concatenate([ratio, ratio * pixel_z], axis=0)), axis=1)
+
+    def over_rows(value):
+        return jnp.sum(value, axis=0, keepdims=True)
 
     def moments(chunk, carry):
-        right = xy_ref[chunk]
+        right = zs_ref[chunk]
         pulled = jnp.dot(left, jnp.concatenate([right, right], axis=0), preferred_element_type=jnp.float32)
         for i in range(CHUNK):
             block = chunk * CHUNK + i
             cols = slice(i * 128, (i + 1) * 128)
-            za = za_ref[block]
-            share = za * pulled[0:rows, cols]
-            mass = over_pixels(share)
-            sum_z = over_pixels(share * pixel_z)
-            sum_x = over_pixels(za * pulled[rows : 2 * rows, cols])
-            sum_y = over_pixels(za * pulled[2 * rows : 3 * rows, cols])
+            xy = xy_ref[block]
+            share = [xy[ix * 8 : ix * 8 + 8] * pulled[ix * 8 : ix * 8 + 8, cols] for ix in range(8)]
+            total = share[7]
+            ramp = share[7]
+            for ix in range(6, 0, -1):
+                total = total + share[ix]
+                ramp = ramp + total
+            total = total + share[0]
+            mass = over_rows(total)
+            sum_x = over_rows(ramp) * 0.125 - mass * (3.5 / 8.0)
+            sum_y = over_rows(total * step8)
+            sum_z = over_rows(jnp.sum((xy * pulled[64:128, cols]).reshape(8, 8, 128), axis=0))
             off_x, off_y = near(block)
             out_ref[block, 0:1, :] = mass
             out_ref[block, 1:2, :] = sum_x - off_x * mass
@@ -209,7 +215,7 @@
     tiles = tile_count // seed_size
     assert tiles * seed_size == tile_count and TILES_Z % tiles == 0
     assert 128 % home_blocks == 0 and lane_count & (lane_count - 1) == 0
-    assert device_count % CHUNK == 0
+    assert device_count % 32 == 0 and 32 % CHUNK == 0
     sizes = (brick_size, seed_size, lane_count, home_blocks)
     vmem = pl.BlockSpec(memory_space=pltpu.VMEM)
     smem = pl.BlockSpec(memory_space=pltpu.SMEM)
@@ -238,16 +244,15 @@
     for turn in range(1, seed_size):
         pairs = [(shard, (shard - turn) % seed_size) for shard in range(seed_size)]
         panels.append(lax.ppermute(own, "seed", pairs))
-    slot_total = own.shape[0] * seed_size
     source, homes = pl.pallas_call(
         functools.partial(prepare_kernel, sizes, tiles),
-        out_shape=(pltpu.VMEM((slot_total, tiles, 128), jnp.int32), pltpu.SMEM((lane_count,), jnp.int32)),
+        out_shape=(pltpu.VMEM((device_count // 32, tiles, 128), jnp.int32), pltpu.SMEM((lane_count,), jnp.int32)),
         in_specs=[vmem] * (2 + seed_size),
         out_specs=(vmem, smem),
         name="prepare",
     )(near(slots), near(cand_count.reshape(1, -1)), *[near(part) for part in panels])
     weight = lax.dynamic_slice_in_dim(pixel_mass, shard_index * tiles, tiles)
-    weight = weight.reshape(tiles, 64, 8).transpose(0, 2, 1).reshape(tiles * 8, 64)
+    weight = weight.reshape(tiles, 64, 8).transpose(1, 0, 2).reshape(64, tiles * 8)
 
     partial = pl.pallas_call(
         functools.partial(main_kernel, tiles),
@@ -256,10 +261,8 @@
         out_specs=vmem,
         scratch_shapes=[
             pltpu.VMEM((device_count, tiles, 128), jnp.float32),
-            pltpu.VMEM((device_count, tiles * 8, 128), jnp.float32),
             pltpu.VMEM((device_count // CHUNK, tiles * 16, CHUNK * 128), jnp.bfloat16),
-            pltpu.VMEM((device_count // CHUNK, 128, CHUNK * 128), jnp.bfloat16),
-            pltpu.VMEM((CHUNK, tiles, 128), jnp.float32),
+            pltpu.VMEM((device_count, 64, 128), jnp.float32),
         ],
         compiler_params=params,
         name="brick_moments",

time: 28.2 us -> 28 us (level)
  no operation moved by 1% of the time
where the time goes in v6:
time: 28 us; the launch traced here: 27.8 us
  blocking collectives  9.1 us (32%)
  starting transfers between devices  7.62 us (27%)
  waiting for transfers between devices  6.22 us (22%)
  Pallas kernels  4.25 us (15%)
  local copies, waits for them, and re-layouts  0.5 us (2%)
    all_to_all x1, blocking collectives, body(): lax.all_to_all(partial, ('brick', 'seed'), split_axis=0, concat_axis=0, t...  9.1 us
    all_to_all x1, starting transfers between devices, body(): lax.all_to_all(outgoing, ('brick', 'seed'), split_axis=0, concat_axis=0,...  7.3 us
    all_to_all x1, waiting for transfers between devices, body(): lax.all_to_all(outgoing, ('brick', 'seed'), split_axis=0, concat_axis=0,...  5.69 us
    pallas_call x1, Pallas kernels, body(): pl.pallas_call(functools.partial(main_kernel, tiles), out_shape=panel, in...  1.69 us
    pallas_call x1, Pallas kernels, body(): pl.pallas_call(functools.partial(pack_kernel, sizes), out_shape=panel, in...  1.59 us
    pallas_call x1, Pallas kernels, body(): pl.pallas_call(functools.partial(place_kernel, seed_size), out_shape=jax....  0.63 us
  transfers between devices with their start and end apart: 2, of which 2 were waited for; matrix products, arithmetic and copies ran while one was open for 1% of the time, Pallas kernels for 1%

profile of v6, /device:TPU:0, one launch (start us, length us, event | category | flops | bytes accessed | tf_op | source)
XLA Modules:
  0.0 27.8 jit_solution(10735172536889743639)
XLA Ops:
  0.0 0.0 copy-start
  0.0 1.6 %pack_seeds.1 = f32[32,4,128]{2,1,0:T(4,128)} custom-call(s32[4,128]{1,0:T(4,128)} %bitcast.5, f32[4,2048]{1,0:T(4,128)} %seeds_hbm.1), custom_call_target="tpu_custom_call" | custom-call | tf_op jit(solution)/shard_map/pack_seeds/pallas_call | solution.py:228
  1.6 0.0 copy-start.2
  1.6 7.3 %all-to-all-start = ((f32[32,4,128]{2,1,0:T(4,128)}), f32[32,4,128]{2,1,0:T(4,128)S(1)}, u32[]{:S(2)}, u32[]{:S(2)}) async-start(f32[32,4,128]{2,1,0:T(4,128)} %pack_seeds.1), calls=%async_computation | async-start | bytes 131072 | tf_op jit(solution)/shard_map/all_to_all | solution.py:240
  8.9 0.0 copy-done.2
  8.9 0.3 %collective-permute-start = (s32[4,16]{1,0:T(4,128)S(1)}, s32[4,16]{1,0:T(4,128)S(1)}, u32[]{:S(2)}, u32[]{:S(2)}) collective-permute-start(s32[4,16]{1,0:T(4,128)S(1)} %bitcast.7), channel_id=1, source_target_pairs={{0,1},{1,0},{2,3},{3,2},{4,5},{5,4},{6,7},{7,6},{8,9},{9,8},{10,11... | collective-permute-start | bytes 776 | tf_op jit(solution)/shard_map/ppermute | solution.py:246
  9.2 0.0 copy-done
  9.3 0.2 reshape.14
  9.4 0.1 copy.6
  9.5 0.0 copy-start.1
  9.5 0.1 copy.7.weight_ref
  9.6 0.0 copy-start.3
  9.6 0.5 %collective-permute-done.refs_1_ = s32[4,16]{1,0:T(4,128)S(1)} collective-permute-done((s32[4,16]{1,0:T(4,128)S(1)}, s32[4,16]{1,0:T(4,128)S(1)}, u32[]{:S(2)}, u32[]{:S(2)}) %collective-permute-start) | collective-permute-done | bytes 288 | tf_op jit(solution)/shard_map/ppermute | solution.py:246
  10.2 0.1 copy-done.1
  10.2 0.1 copy-done.3
  10.3 0.3 %prepare.1 = (s32[1,8,128]{2,1,0:T(8,128)S(1)}, s32[16]{0:T(128)S(4)}) custom-call(s32[4,128]{1,0:T(4,128)S(1)} %bitcast.6, s32[1,16]{1,0:T(1,128)S(1)} %bitcast.9, s32[4,16]{1,0:T(4,128)S(1)} %bitcast.8, s32[4,16]{1,0:T(4,128)S(1)} %collective-permute-done.refs_1_), custom_call_target="tpu_custom_call" | custom-call | tf_op jit(solution)/shard_map/prepare/pallas_call | solution.py:247
  10.6 5.7 %all-to-all-done.seeds_ref = f32[32,4,128]{2,1,0:T(4,128)S(1)} async-done(((f32[32,4,128]{2,1,0:T(4,128)}), f32[32,4,128]{2,1,0:T(4,128)S(1)}, u32[]{:S(2)}, u32[]{:S(2)}) %all-to-all-start) | async-done | bytes 65568 | tf_op jit(solution)/shard_map/all_to_all | solution.py:240
  16.3 1.7 %brick_moments.1 = f32[32,4,128]{2,1,0:T(4,128)S(1)} custom-call(s32[1,8,128]{2,1,0:T(8,128)S(1)} %get-tuple-element.8.source_ref, f32[64,64]{1,0:T(8,128)S(1)} %copy.7.weight_ref, f32[32,4,128]{2,1,0:T(4,128)S(1)} %all-to-all-done.seeds_ref), custom_call_target="tpu_custom_call" | custom-call | tf_op jit(solution)/shard_map/brick_moments/pallas_call | solution.py:257
  18.0 9.1 %all_to_all.10.partial_ref = f32[32,4,128]{2,1,0:T(4,128)S(1)} all-to-all(f32[32,4,128]{2,1,0:T(4,128)S(1)} %brick_moments.1), channel_id=1, replica_groups=mesh['brick'=16,'seed'=2] {'brick','seed'}, dimensions={0} | all-to-all | bytes 131072 | tf_op jit(solution)/shard_map/all_to_all | solution.py:270
  27.1 0.6 %place_stats.1 = f32[4,2048]{1,0:T(4,128)} custom-call(s32[16]{0:T(128)S(4)} %get-tuple-element.7.homes_ref, f32[32,4,128]{2,1,0:T(4,128)S(1)} %all_to_all.10.partial_ref), custom_call_target="tpu_custom_call" | custom-call | tf_op jit(solution)/shard_map/place_stats/pallas_call | solution.py:271
  (1 shorter events, 0.0 us)
Async XLA Ops:
  0.0 9.2 %copy-start = (f32[16,512]{1,0:T(8,128)S(1)}, f32[16,512]{1,0:T(8,128)}, u32[]{:S(2)}) copy-start(f32[16,512]{1,0:T(8,128)} %param.9) | copy-start | bytes 98308
  1.6 7.3 %copy-start.2 = (s32[16,4]{0,1:T(4,128)S(1)}, s32[16,4]{0,1:T(4,128)}, u32[]{:S(2)}) copy-start(s32[16,4]{0,1:T(4,128)} %param.7) | copy-start | bytes 772
  1.6 14.7 %all-to-all-start = ((f32[32,4,128]{2,1,0:T(4,128)}), f32[32,4,128]{2,1,0:T(4,128)S(1)}, u32[]{:S(2)}, u32[]{:S(2)}) async-start(f32[32,4,128]{2,1,0:T(4,128)} %pack_seeds.1), calls=%async_computation | async-start | bytes 131072 | tf_op jit(solution)/shard_map/all_to_all | solution.py:240
  8.9 1.2 %collective-permute-start = (s32[4,16]{1,0:T(4,128)S(1)}, s32[4,16]{1,0:T(4,128)S(1)}, u32[]{:S(2)}, u32[]{:S(2)}) collective-permute-start(s32[4,16]{1,0:T(4,128)S(1)} %bitcast.7), channel_id=1, source_target_pairs={{0,1},{1,0},{2,3},{3,2},{4,5},{5,4},{6,7},{7,6},{8,9},{9,8},{10,11... | collective-permute-start | bytes 776 | tf_op jit(solution)/shard_map/ppermute | solution.py:246
  9.5 0.7 %copy-start.1 = (s32[512]{0:T(512)S(1)}, s32[512]{0:T(512)}, u32[]{:S(2)}) copy-start(s32[512]{0:T(512)} %param.6) | copy-start | bytes 6148
  9.6 0.7 %copy-start.3 = (s32[16]{0:T(128)S(1)}, s32[16]{0:T(128)}, u32[]{:S(2)}) copy-start(s32[16]{0:T(128)} %param.8) | copy-start | bytes 196

commit v7 on v6

--- a/solution.py
+++ b/solution.py
@@ -41,7 +41,7 @@
         first = pl.multiple_of(jnp.maximum(lanes[home], 0) * 128, 128)
         block = jnp.where(lanes[home] >= 0, seeds_ref[:, pl.ds(first, 128)], 0.0)
         for shard in range(seed_size):
-            out_ref[home * seed_size + shard] = block
+            out_ref[shard * brick_size + home] = block
 
 
 def prepare_kernel(sizes, tiles, slots_ref, counts_ref, *refs):
@@ -55,7 +55,9 @@
     row = brick_index // (128 // home_blocks)
     lanes = lax.broadcasted_iota(jnp.int32, (1, 128), 1)
     ident = jnp.broadcast_to(row * 128 + lanes, (tiles, 128))
-    holder = jnp.broadcast_to(slots_ref[pl.ds(row, 1), :] >> shift, (tiles, 128))
+    holder = slots_ref[pl.ds(row, 1), :] >> shift
+    holder = (holder & (seed_size - 1)) * brick_size + (holder >> (seed_size.bit_length() - 1))
+    holder = jnp.broadcast_to(holder, (tiles, 128))
     mine = shard_index * tiles + lax.broadcasted_iota(jnp.int32, (tiles, tile_count), 0)
     mine = mine == lax.broadcasted_iota(jnp.int32, (tiles, tile_count), 1)
     counts = counts_ref[...]
@@ -83,12 +85,12 @@
         homes_ref[lane] = jnp.max(jnp.where(slots == first + lane, home, 0))
 
 
-def place_kernel(seed_size, homes_ref, partial_ref, out_ref):
+def place_kernel(brick_size, seed_size, homes_ref, partial_ref, out_ref):
     for lane in range(out_ref.shape[1] // 128):
-        first = homes_ref[lane] * seed_size
-        block = partial_ref[first]
+        home = homes_ref[lane]
+        block = partial_ref[home]
         for shard in range(1, seed_size):
-            block = block + partial_ref[first + shard]
+            block = block + partial_ref[shard * brick_size + home]
         out_ref[:, lane * 128 : (lane + 1) * 128] = block
 
 
@@ -214,6 +216,7 @@
     tile_count = candidates.shape[0]
     tiles = tile_count // seed_size
     assert tiles * seed_size == tile_count and TILES_Z % tiles == 0
+    assert seed_size & (seed_size - 1) == 0
     assert 128 % home_blocks == 0 and lane_count & (lane_count - 1) == 0
     assert device_count % 32 == 0 and 32 % CHUNK == 0
     sizes = (brick_size, seed_size, lane_count, home_blocks)
@@ -237,7 +240,7 @@
         ],
         name="pack_seeds",
     )(slots, seed_data)
-    incoming = lax.all_to_all(outgoing, ("brick", "seed"), split_axis=0, concat_axis=0, tiled=True)
+    incoming = lax.all_to_all(outgoing, ("seed", "brick"), split_axis=0, concat_axis=0, tiled=True)
 
     own = candidates.T
     panels = [own]
@@ -267,9 +270,9 @@
         compiler_params=params,
         name="brick_moments",
     )(near(source), near(weight), near(incoming))
-    returned = lax.all_to_all(partial, ("brick", "seed"), split_axis=0, concat_axis=0, tiled=True)
+    returned = lax.all_to_all(partial, ("seed", "brick"), split_axis=0, concat_axis=0, tiled=True)
     return pl.pallas_call(
-        functools.partial(place_kernel, seed_size),
+        functools.partial(place_kernel, brick_size, seed_size),
         out_shape=jax.ShapeDtypeStruct(seed_data.shape, jnp.float32),
         in_specs=[smem, vmem],
         out_specs=vmem,

time: 28 us -> 27.9 us (level)
  no operation moved by 1% of the time
where the time goes in v7:
time: 27.9 us; the launch traced here: 27.6 us
  blocking collectives  9.02 us (32%)
  starting transfers between devices  7.62 us (27%)
  waiting for transfers between devices  6.13 us (22%)
  Pallas kernels  4.26 us (15%)
  local copies, waits for them, and re-layouts  0.5 us (2%)
    all_to_all x1, blocking collectives, body(): lax.all_to_all(partial, ('seed', 'brick'), split_axis=0, concat_axis=0, t...  9.02 us
    all_to_all x1, starting transfers between devices, body(): lax.all_to_all(outgoing, ('seed', 'brick'), split_axis=0, concat_axis=0,...  7.3 us
    all_to_all x1, waiting for transfers between devices, body(): lax.all_to_all(outgoing, ('seed', 'brick'), split_axis=0, concat_axis=0,...  5.61 us
    pallas_call x1, Pallas kernels, body(): pl.pallas_call(functools.partial(main_kernel, tiles), out_shape=panel, in...  1.69 us
    pallas_call x1, Pallas kernels, body(): pl.pallas_call(functools.partial(pack_kernel, sizes), out_shape=panel, in...  1.59 us
    pallas_call x1, Pallas kernels, body(): pl.pallas_call(functools.partial(place_kernel, brick_size, seed_size), ou...  0.63 us
  transfers between devices with their start and end apart: 2, of which 2 were waited for; matrix products, arithmetic and copies ran while one was open for 1% of the time, Pallas kernels for 1%

profile of v7, /device:TPU:0, one launch (start us, length us, event | category | flops | bytes accessed | tf_op | source)
XLA Modules:
  0.0 27.6 jit_solution(12817005186798926705)
XLA Ops:
  0.0 0.0 copy-start
  0.0 1.6 %pack_seeds.1 = f32[32,4,128]{2,1,0:T(4,128)} custom-call(s32[4,128]{1,0:T(4,128)} %bitcast.5, f32[4,2048]{1,0:T(4,128)} %seeds_hbm.1), custom_call_target="tpu_custom_call" | custom-call | tf_op jit(solution)/shard_map/pack_seeds/pallas_call | solution.py:231
  1.6 0.0 copy-start.2
  1.6 7.3 %all-to-all-start = ((f32[32,4,128]{2,1,0:T(4,128)}), f32[32,4,128]{2,1,0:T(4,128)S(1)}, u32[]{:S(2)}, u32[]{:S(2)}) async-start(f32[32,4,128]{2,1,0:T(4,128)} %pack_seeds.1), calls=%async_computation | async-start | bytes 131072 | tf_op jit(solution)/shard_map/all_to_all | solution.py:243
  8.9 0.0 copy-done.2
  8.9 0.3 %collective-permute-start = (s32[4,16]{1,0:T(4,128)S(1)}, s32[4,16]{1,0:T(4,128)S(1)}, u32[]{:S(2)}, u32[]{:S(2)}) collective-permute-start(s32[4,16]{1,0:T(4,128)S(1)} %bitcast.7), channel_id=1, source_target_pairs={{0,1},{1,0},{2,3},{3,2},{4,5},{5,4},{6,7},{7,6},{8,9},{9,8},{10,11... | collective-permute-start | bytes 776 | tf_op jit(solution)/shard_map/ppermute | solution.py:249
  9.2 0.0 copy-done
  9.3 0.2 reshape.14
  9.4 0.1 copy.6
  9.5 0.0 copy-start.1
  9.5 0.1 copy.7.weight_ref
  9.6 0.0 copy-start.3
  9.6 0.5 %collective-permute-done.refs_1_ = s32[4,16]{1,0:T(4,128)S(1)} collective-permute-done((s32[4,16]{1,0:T(4,128)S(1)}, s32[4,16]{1,0:T(4,128)S(1)}, u32[]{:S(2)}, u32[]{:S(2)}) %collective-permute-start) | collective-permute-done | bytes 288 | tf_op jit(solution)/shard_map/ppermute | solution.py:249
  10.2 0.1 copy-done.1
  10.2 0.1 copy-done.3
  10.3 0.3 %prepare.1 = (s32[1,8,128]{2,1,0:T(8,128)S(1)}, s32[16]{0:T(128)S(4)}) custom-call(s32[4,128]{1,0:T(4,128)S(1)} %bitcast.6, s32[1,16]{1,0:T(1,128)S(1)} %bitcast.9, s32[4,16]{1,0:T(4,128)S(1)} %bitcast.8, s32[4,16]{1,0:T(4,128)S(1)} %collective-permute-done.refs_1_), custom_call_target="tpu_custom_call" | custom-call | tf_op jit(solution)/shard_map/prepare/pallas_call | solution.py:250
  10.6 5.6 %all-to-all-done.seeds_ref = f32[32,4,128]{2,1,0:T(4,128)S(1)} async-done(((f32[32,4,128]{2,1,0:T(4,128)}), f32[32,4,128]{2,1,0:T(4,128)S(1)}, u32[]{:S(2)}, u32[]{:S(2)}) %all-to-all-start) | async-done | bytes 65568 | tf_op jit(solution)/shard_map/all_to_all | solution.py:243
  16.2 1.7 %brick_moments.1 = f32[32,4,128]{2,1,0:T(4,128)S(1)} custom-call(s32[1,8,128]{2,1,0:T(8,128)S(1)} %get-tuple-element.8.source_ref, f32[64,64]{1,0:T(8,128)S(1)} %copy.7.weight_ref, f32[32,4,128]{2,1,0:T(4,128)S(1)} %all-to-all-done.seeds_ref), custom_call_target="tpu_custom_call" | custom-call | tf_op jit(solution)/shard_map/brick_moments/pallas_call | solution.py:260
  17.9 9.0 %all_to_all.10.partial_ref = f32[32,4,128]{2,1,0:T(4,128)S(1)} all-to-all(f32[32,4,128]{2,1,0:T(4,128)S(1)} %brick_moments.1), channel_id=1, replica_groups=mesh['brick'=16,'seed'=2] {'seed','brick'}, dimensions={0} | all-to-all | bytes 131072 | tf_op jit(solution)/shard_map/all_to_all | solution.py:273
  27.0 0.6 %place_stats.1 = f32[4,2048]{1,0:T(4,128)} custom-call(s32[16]{0:T(128)S(4)} %get-tuple-element.7.homes_ref, f32[32,4,128]{2,1,0:T(4,128)S(1)} %all_to_all.10.partial_ref), custom_call_target="tpu_custom_call" | custom-call | tf_op jit(solution)/shard_map/place_stats/pallas_call | solution.py:274
  (1 shorter events, 0.0 us)
Async XLA Ops:
  0.0 9.2 %copy-start = (f32[16,512]{1,0:T(8,128)S(1)}, f32[16,512]{1,0:T(8,128)}, u32[]{:S(2)}) copy-start(f32[16,512]{1,0:T(8,128)} %param.9) | copy-start | bytes 98308
  1.6 7.3 %copy-start.2 = (s32[16,4]{0,1:T(4,128)S(1)}, s32[16,4]{0,1:T(4,128)}, u32[]{:S(2)}) copy-start(s32[16,4]{0,1:T(4,128)} %param.7) | copy-start | bytes 772
  1.6 14.6 %all-to-all-start = ((f32[32,4,128]{2,1,0:T(4,128)}), f32[32,4,128]{2,1,0:T(4,128)S(1)}, u32[]{:S(2)}, u32[]{:S(2)}) async-start(f32[32,4,128]{2,1,0:T(4,128)} %pack_seeds.1), calls=%async_computation | async-start | bytes 131072 | tf_op jit(solution)/shard_map/all_to_all | solution.py:243
  8.9 1.2 %collective-permute-start = (s32[4,16]{1,0:T(4,128)S(1)}, s32[4,16]{1,0:T(4,128)S(1)}, u32[]{:S(2)}, u32[]{:S(2)}) collective-permute-start(s32[4,16]{1,0:T(4,128)S(1)} %bitcast.7), channel_id=1, source_target_pairs={{0,1},{1,0},{2,3},{3,2},{4,5},{5,4},{6,7},{7,6},{8,9},{9,8},{10,11... | collective-permute-start | bytes 776 | tf_op jit(solution)/shard_map/ppermute | solution.py:249
  9.5 0.7 %copy-start.1 = (s32[512]{0:T(512)S(1)}, s32[512]{0:T(512)}, u32[]{:S(2)}) copy-start(s32[512]{0:T(512)} %param.6) | copy-start | bytes 6148
  9.6 0.7 %copy-start.3 = (s32[16]{0:T(128)S(1)}, s32[16]{0:T(128)}, u32[]{:S(2)}) copy-start(s32[16]{0:T(128)} %param.8) | copy-start | bytes 196

commit v8 on v7

--- a/solution.py
+++ b/solution.py
@@ -13,7 +13,7 @@
 LOG2E = 1.4426950408889634
 LIFT = 40.0
 DEAD = -1e30
-CHUNK = 4
+CHUNK = 8
 
 
 def stored_lane(slots, home, lane_count, home_blocks, device_index):
@@ -165,7 +165,7 @@
         second = dot(jnp.concatenate(planes[half:], axis=1), jnp.concatenate(columns[half:], axis=1))
         return totals[0] + first, totals[1] + second
 
-    totals = lax.fori_loop(0, chunk_count, factors, (jnp.zeros((128, 2 * rows), jnp.float32),) * 2, unroll=8)
+    totals = lax.fori_loop(0, chunk_count, factors, (jnp.zeros((128, 2 * rows), jnp.float32),) * 2, unroll=4)
     totals = totals[0] + totals[1]
     totals = totals[0:64] + totals[64:128]
     totals = totals[:, 0:rows] + totals[:, rows : 2 * rows]
@@ -203,7 +203,7 @@
             out_ref[block, 3:4, :] = sum_z - seeds_ref[block, 2:3, :] * mass
         return carry
 
-    lax.fori_loop(0, chunk_count, moments, 0, unroll=8)
+    lax.fori_loop(0, chunk_count, moments, 0, unroll=4)
 
 
 def body(seed_data, block_slot, candidates, cand_count, pixel_mass):

time: 27.9 us -> 27.9 us (level)
  no operation moved by 1% of the time
where the time goes in v8:
time: 27.9 us; the launch traced here: 27.6 us
  blocking collectives  9.02 us (32%)
  starting transfers between devices  7.62 us (27%)
  waiting for transfers between devices  6.13 us (22%)
  Pallas kernels  4.26 us (15%)
  local copies, waits for them, and re-layouts  0.5 us (2%)
    all_to_all x1, blocking collectives, body(): lax.all_to_all(partial, ('seed', 'brick'), split_axis=0, concat_axis=0, t...  9.02 us
    all_to_all x1, starting transfers between devices, body(): lax.all_to_all(outgoing, ('seed', 'brick'), split_axis=0, concat_axis=0,...  7.3 us
    all_to_all x1, waiting for transfers between devices, body(): lax.all_to_all(outgoing, ('seed', 'brick'), split_axis=0, concat_axis=0,...  5.61 us
    pallas_call x1, Pallas kernels, body(): pl.pallas_call(functools.partial(main_kernel, tiles), out_shape=panel, in...  1.7 us
    pallas_call x1, Pallas kernels, body(): pl.pallas_call(functools.partial(pack_kernel, sizes), out_shape=panel, in...  1.59 us
    pallas_call x1, Pallas kernels, body(): pl.pallas_call(functools.partial(place_kernel, brick_size, seed_size), ou...  0.63 us
  transfers between devices with their start and end apart: 2, of which 2 were waited for; matrix products, arithmetic and copies ran while one was open for 1% of the time, Pallas kernels for 1%

profile of v8, /device:TPU:0, one launch (start us, length us, event | category | flops | bytes accessed | tf_op | source)
XLA Modules:
  0.0 27.6 jit_solution(8376466920983306128)
XLA Ops:
  0.0 0.0 copy-start
  0.0 1.6 %pack_seeds.1 = f32[32,4,128]{2,1,0:T(4,128)} custom-call(s32[4,128]{1,0:T(4,128)} %bitcast.5, f32[4,2048]{1,0:T(4,128)} %seeds_hbm.1), custom_call_target="tpu_custom_call" | custom-call | tf_op jit(solution)/shard_map/pack_seeds/pallas_call | solution.py:231
  1.6 0.0 copy-start.2
  1.6 7.3 %all-to-all-start = ((f32[32,4,128]{2,1,0:T(4,128)}), f32[32,4,128]{2,1,0:T(4,128)S(1)}, u32[]{:S(2)}, u32[]{:S(2)}) async-start(f32[32,4,128]{2,1,0:T(4,128)} %pack_seeds.1), calls=%async_computation | async-start | bytes 131072 | tf_op jit(solution)/shard_map/all_to_all | solution.py:243
  8.9 0.0 copy-done.2
  8.9 0.3 %collective-permute-start = (s32[4,16]{1,0:T(4,128)S(1)}, s32[4,16]{1,0:T(4,128)S(1)}, u32[]{:S(2)}, u32[]{:S(2)}) collective-permute-start(s32[4,16]{1,0:T(4,128)S(1)} %bitcast.7), channel_id=1, source_target_pairs={{0,1},{1,0},{2,3},{3,2},{4,5},{5,4},{6,7},{7,6},{8,9},{9,8},{10,11... | collective-permute-start | bytes 776 | tf_op jit(solution)/shard_map/ppermute | solution.py:249
  9.2 0.0 copy-done
  9.3 0.2 reshape.14
  9.4 0.1 copy.6
  9.5 0.0 copy-start.1
  9.5 0.1 copy.7.weight_ref
  9.6 0.0 copy-start.3
  9.6 0.5 %collective-permute-done.refs_1_ = s32[4,16]{1,0:T(4,128)S(1)} collective-permute-done((s32[4,16]{1,0:T(4,128)S(1)}, s32[4,16]{1,0:T(4,128)S(1)}, u32[]{:S(2)}, u32[]{:S(2)}) %collective-permute-start) | collective-permute-done | bytes 288 | tf_op jit(solution)/shard_map/ppermute | solution.py:249
  10.2 0.1 copy-done.1
  10.2 0.1 copy-done.3
  10.3 0.3 %prepare.1 = (s32[1,8,128]{2,1,0:T(8,128)S(1)}, s32[16]{0:T(128)S(4)}) custom-call(s32[4,128]{1,0:T(4,128)S(1)} %bitcast.6, s32[1,16]{1,0:T(1,128)S(1)} %bitcast.9, s32[4,16]{1,0:T(4,128)S(1)} %bitcast.8, s32[4,16]{1,0:T(4,128)S(1)} %collective-permute-done.refs_1_), custom_call_target="tpu_custom_call" | custom-call | tf_op jit(solution)/shard_map/prepare/pallas_call | solution.py:250
  10.6 5.6 %all-to-all-done.seeds_ref = f32[32,4,128]{2,1,0:T(4,128)S(1)} async-done(((f32[32,4,128]{2,1,0:T(4,128)}), f32[32,4,128]{2,1,0:T(4,128)S(1)}, u32[]{:S(2)}, u32[]{:S(2)}) %all-to-all-start) | async-done | bytes 65568 | tf_op jit(solution)/shard_map/all_to_all | solution.py:243
  16.2 1.7 %brick_moments.1 = f32[32,4,128]{2,1,0:T(4,128)S(1)} custom-call(s32[1,8,128]{2,1,0:T(8,128)S(1)} %get-tuple-element.8.source_ref, f32[64,64]{1,0:T(8,128)S(1)} %copy.7.weight_ref, f32[32,4,128]{2,1,0:T(4,128)S(1)} %all-to-all-done.seeds_ref), custom_call_target="tpu_custom_call" | custom-call | tf_op jit(solution)/shard_map/brick_moments/pallas_call | solution.py:260
  17.9 9.0 %all_to_all.10.partial_ref = f32[32,4,128]{2,1,0:T(4,128)S(1)} all-to-all(f32[32,4,128]{2,1,0:T(4,128)S(1)} %brick_moments.1), channel_id=1, replica_groups=mesh['brick'=16,'seed'=2] {'seed','brick'}, dimensions={0} | all-to-all | bytes 131072 | tf_op jit(solution)/shard_map/all_to_all | solution.py:273
  27.0 0.6 %place_stats.1 = f32[4,2048]{1,0:T(4,128)} custom-call(s32[16]{0:T(128)S(4)} %get-tuple-element.7.homes_ref, f32[32,4,128]{2,1,0:T(4,128)S(1)} %all_to_all.10.partial_ref), custom_call_target="tpu_custom_call" | custom-call | tf_op jit(solution)/shard_map/place_stats/pallas_call | solution.py:274
  (1 shorter events, 0.0 us)
Async XLA Ops:
  0.0 9.2 %copy-start = (f32[16,512]{1,0:T(8,128)S(1)}, f32[16,512]{1,0:T(8,128)}, u32[]{:S(2)}) copy-start(f32[16,512]{1,0:T(8,128)} %param.9) | copy-start | bytes 98308
  1.6 7.3 %copy-start.2 = (s32[16,4]{0,1:T(4,128)S(1)}, s32[16,4]{0,1:T(4,128)}, u32[]{:S(2)}) copy-start(s32[16,4]{0,1:T(4,128)} %param.7) | copy-start | bytes 772
  1.6 14.6 %all-to-all-start = ((f32[32,4,128]{2,1,0:T(4,128)}), f32[32,4,128]{2,1,0:T(4,128)S(1)}, u32[]{:S(2)}, u32[]{:S(2)}) async-start(f32[32,4,128]{2,1,0:T(4,128)} %pack_seeds.1), calls=%async_computation | async-start | bytes 131072 | tf_op jit(solution)/shard_map/all_to_all | solution.py:243
  8.9 1.2 %collective-permute-start = (s32[4,16]{1,0:T(4,128)S(1)}, s32[4,16]{1,0:T(4,128)S(1)}, u32[]{:S(2)}, u32[]{:S(2)}) collective-permute-start(s32[4,16]{1,0:T(4,128)S(1)} %bitcast.7), channel_id=1, source_target_pairs={{0,1},{1,0},{2,3},{3,2},{4,5},{5,4},{6,7},{7,6},{8,9},{9,8},{10,11... | collective-permute-start | bytes 776 | tf_op jit(solution)/shard_map/ppermute | solution.py:249
  9.5 0.7 %copy-start.1 = (s32[512]{0:T(512)S(1)}, s32[512]{0:T(512)}, u32[]{:S(2)}) copy-start(s32[512]{0:T(512)} %param.6) | copy-start | bytes 6148
  9.6 0.7 %copy-start.3 = (s32[16]{0:T(128)S(1)}, s32[16]{0:T(128)}, u32[]{:S(2)}) copy-start(s32[16]{0:T(128)} %param.8) | copy-start | bytes 196
